TPU v7x, 32 devices: a whole 2x2x4 slice. The times are simulated.
32 devices in a mesh: grp: 16 (over z, y, x), lag: 2 (over core).
Axes of the slice: x: 2, y: 2, z: 4, core: 2. Of those that a mesh axis runs over, the one named last changes fastest.
Arguments:
- waveforms: float32 [256, 8, 2048], P('grp'), may hold values from -6 to 6
- pair_bin: int32 [256, 256], P('grp'), may hold values from 0 to 127, as said below
Outputs:
- stack: float32 [128, 1024], P('grp', 'lag')
Inputs may be any that keep to these rules, and one draw needn't show every extreme that they name: pair_bin is symmetric: the bin of stations i and j is that of j and i.
All inputs are finite; a program needn't handle non-finite values.
Results may differ from a plain program's by a relative error of at most 0.0049.
Values may be sent and summed in bfloat16 or wider, within the bound.
No kernel may reach another device: no remote copies, remote signals or barrier semaphores. Data moves between devices by JAX's collectives and lax.ppermute only.
A program may use at most 64 MiB of HBM per device.

v0:
```python
import math

import jax
import jax.numpy as jnp
from jax import lax
from jax.sharding import PartitionSpec as P

NFFT = 2048
LAGS = 1024
HW = 32
BIN_DEV = 8


EPSILON = 1e-06


def with_halo(block, sides, width):
    for axis, dim in sides:
        count = lax.axis_size(axis)
        forward = [(i, i + 1) for i in range(count - 1)]
        backward = [(target, source) for source, target in forward]
        low = lax.ppermute(
            lax.slice_in_dim(block, block.shape[dim] - width, None, axis=dim), axis, forward
        )
        high = lax.ppermute(lax.slice_in_dim(block, 0, width, axis=dim), axis, backward)
        block = jnp.concatenate([low, block, high], axis=dim)
    return block


def forward_table(freq_start, freq_count):
    sample_index = jnp.arange(NFFT, dtype=jnp.int32)[:, None]
    bin_index = freq_start + jnp.arange(freq_count, dtype=jnp.int32)[None, :]
    phase = (sample_index * bin_index % NFFT).astype(jnp.float32) * (2.0 * math.pi / NFFT)
    return jnp.concatenate([jnp.cos(phase), -jnp.sin(phase)], axis=1)


def inverse_table(freq_start, freq_count):
    bin_index = freq_start + jnp.arange(freq_count, dtype=jnp.int32)
    shifted = jnp.arange(LAGS, dtype=jnp.int32) - LAGS // 2
    phase = (bin_index[:, None] * shifted[None, :] % NFFT).astype(jnp.float32) * (
        2.0 * math.pi / NFFT
    )
    weight = jnp.where(bin_index == 0, 1.0, 2.0).astype(jnp.float32)[:, None] / NFFT
    return jnp.concatenate([weight * jnp.cos(phase), -weight * jnp.sin(phase)], axis=0)


def window_band(freq_count):
    padded_index = jnp.arange(freq_count + 2 * HW, dtype=jnp.int32)[:, None]
    bin_index = jnp.arange(freq_count, dtype=jnp.int32)[None, :]
    inside = (padded_index >= bin_index) & (padded_index <= bin_index + 2 * HW)
    return inside.astype(jnp.float32)


def window_count(freq_start, freq_count, half_length):
    bin_index = freq_start + jnp.arange(freq_count, dtype=jnp.int32)
    upper = jnp.minimum(bin_index + HW, half_length - 1)
    lower = jnp.maximum(bin_index - HW, 0)
    return (upper - lower + 1).astype(jnp.float32)


def add_block(running, whitened, remote, column_start, keep_pairs, imag_sign, pair_bin):
    freq_count = whitened.shape[2] // 2
    row_count = whitened.shape[0]
    column_count = remote.shape[0]
    own_real = whitened[..., :freq_count]
    own_imag = whitened[..., freq_count:]
    far_real = remote[..., :freq_count]
    far_imag = remote[..., freq_count:]
    own_stack = jnp.concatenate([own_real, own_imag], axis=1)
    own_alt = jnp.concatenate([own_real, -own_imag], axis=1)
    far_stack = jnp.concatenate([far_real, far_imag], axis=1)
    far_alt = jnp.concatenate([far_imag, far_real], axis=1)
    real_sum = jnp.einsum("asf,bsf->abf", own_stack, far_stack, preferred_element_type=jnp.float32)
    imag_sum = (
        jnp.einsum("asf,bsf->abf", own_alt, far_alt, preferred_element_type=jnp.float32) * imag_sign
    )
    cross = jnp.concatenate([real_sum, imag_sum], axis=2).astype(jnp.bfloat16)
    cross = cross.reshape(row_count * column_count, 2 * freq_count)
    block_bins = lax.dynamic_slice_in_dim(pair_bin, column_start, column_count, 1)
    block_bins = jnp.where(keep_pairs, block_bins, -1).reshape(-1)
    onehot = (block_bins[None, :] == jnp.arange(running.shape[0], dtype=jnp.int32)[:, None]).astype(
        jnp.bfloat16
    )
    return running + jnp.dot(onehot, cross, preferred_element_type=jnp.float32)


def local(waveforms, pair_bin):
    station_count = waveforms.shape[0]
    segments = waveforms.shape[1]
    groups = lax.axis_size("grp")
    group_index = lax.axis_index("grp")
    half_length = NFFT // 2
    freq_count = half_length // lax.axis_size("lag")
    freq_start = lax.axis_index("lag") * freq_count
    spectra = jnp.dot(
        waveforms.reshape(station_count * segments, NFFT),
        forward_table(freq_start, freq_count),
        precision=lax.Precision.HIGHEST,
        preferred_element_type=jnp.float32,
    )
    spectra = spectra.reshape(station_count, segments, 2 * freq_count)
    real_part = spectra[..., :freq_count]
    imag_part = spectra[..., freq_count:]
    amplitude = jnp.sqrt(real_part * real_part + imag_part * imag_part)
    padded = with_halo(amplitude, (("lag", 2),), HW)
    smoothed = jnp.dot(
        padded.reshape(station_count * segments, freq_count + 2 * HW),
        window_band(freq_count),
        precision=lax.Precision.HIGHEST,
        preferred_element_type=jnp.float32,
    )
    smoothed = smoothed.reshape(station_count, segments, freq_count) / window_count(
        freq_start, freq_count, half_length
    )
    whitened = jnp.concatenate(
        [real_part / (smoothed + EPSILON), imag_part / (smoothed + EPSILON)], axis=2
    ).astype(jnp.bfloat16)
    bins_total = BIN_DEV * groups
    row_start = group_index * station_count
    initial = jnp.zeros((bins_total, 2 * freq_count), jnp.float32)
    local_rows = jnp.arange(station_count, dtype=jnp.int32)
    remote = lax.all_gather(whitened, "grp", axis=0, tiled=True)
    group_total = remote.shape[0] // station_count
    per_step = max((divisor for divisor in (4, 3, 2, 1) if group_total % divisor == 0))
    step_count = group_total // per_step
    block_width = per_step * station_count
    blocks = remote.reshape(step_count, block_width, remote.shape[1], remote.shape[2])

    def one_step(step_index, carried):
        column_block = lax.dynamic_index_in_dim(blocks, step_index, 0, keepdims=False)
        column_start = step_index * block_width
        column_index = column_start + jnp.arange(block_width, dtype=jnp.int32)
        keep_pairs = column_index[None, :] > (row_start + local_rows)[:, None]

        def compute(accumulated):
            return add_block(
                accumulated, whitened, column_block, column_start, keep_pairs, 1.0, pair_bin
            )

        return lax.cond(
            column_start + block_width > row_start,
            compute,
            lambda accumulated: accumulated,
            carried,
        )

    binned = lax.fori_loop(0, step_count, one_step, initial)
    inverse = inverse_table(freq_start, freq_count)
    owned_bins = lax.psum_scatter(binned, "grp", scatter_dimension=0, tiled=True)
    lag_partial = jnp.dot(
        owned_bins, inverse, precision=lax.Precision.HIGHEST, preferred_element_type=jnp.float32
    )
    return lax.psum_scatter(lag_partial, "lag", scatter_dimension=1, tiled=True)


def solution(mesh):
    in_specs = (P("grp", None, None), P("grp", None))
    out_specs = P("grp", "lag")
    return jax.shard_map(local, mesh=mesh, in_specs=in_specs, out_specs=out_specs, check_vma=False)
```

profile of v0, /device:TPU:0, one launch (start us, length us, event | category | flops | bytes accessed | tf_op | source)
XLA Modules:
  0.0 322.4 jit_solution(7806394600709355711)
XLA Ops:
  6.5 16.7 %fusion.42 = (f32[2048,512]{1,0:T(8,128)S(1)}, f32[2048,512]{1,0:T(8,128)S(1)}) fusion(s32[512]{0:T(512)S(1)} %iota_add_fusion.2), kind=kLoop, calls=%fused_computation.56 | loop fusion | flops 15728640 | bytes 8390656 | tf_op jit(solution)/shard_map/cos | solution.py:34
  23.2 4.7 %fusion.43 = f32[16,8,1024]{2,1,0:T(8,128)S(1)} fusion(f32[2048,512]{1,0:T(8,128)S(1)} %get-tuple-element.295, f32[2048,512]{1,0:T(8,128)S(1)} %get-tuple-element.294, f32[16,8,2048]{2,1,0:T(8,128)S(1)} %copy-done), kind=kOutput, calls=%fused_computation.59 | convolution fusion | flops 3223322624 | bytes 9961472 | tf_op jit(solution)/shard_map/dot_general | solution.py:95
  35.1 78.3 %all-gather.2.cloned.1.call-done = bf16[256,8,1024]{2,1,0:T(8,128)(2,1)} async-done(((bf16[16,8,1024]{2,1,0:T(8,128)(2,1)}), bf16[256,8,1024]{2,1,0:T(8,128)(2,1)}) %all-gather.2.cloned.1.call-update) | async-done | bytes 4194320 | tf_op jit(solution)/shard_map/all_gather | solution.py:122
  113.4 11.8 %copy.13 = bf16[4,64,8,1024]{1,2,3,0:T(8,128)(2,1)} copy(bf16[4,64,8,1024]{3,2,1,0:T(8,128)(2,1)} %bitcast.32) | data formatting | bytes 8388608
  126.0 107.5 %while.17 = (s32[]{:T(128)}, f32[128,1024]{1,0:T(8,128)}, s32[]{:T(128)}, s32[16,256]{1,0:T(8,128)S(1)}, bf16[4,64,8,1024]{1,2,3,0:T(8,128)(2,1)}, /*index=5*/bf16[16,8,1024]{2,1,0:T(8,128)(2,1)}, s32[]{:T(128)}, s32[]{:T(128)}) while((s32[]{:T(128)}, f32[128,1024]{1,0:T(8,128)}, s32[]{:T(128)}, s32[16,256]{1,0:T(8,128)S(1)}, ...), condition=%wide.region_3.4_spmd.clone, body=%wide.region_0.3_spmd.clone.sunk | while | flops 312674400 | bytes 23090748 | solution.py:147
  126.0 26.9 %conditional.3 = (f32[128,1024]{1,0:T(8,128)}) conditional(s32[]{:T(128)} %convert_element_type.47, f32[128,1024]{1,0:T(8,128)} %get-tuple-element.346, (s32[]{:T(128)}, s32[1,64]{1,0:T(1,128)S(1)}, s32[]{:T(128)}, s32[16]{0:T(128)S(1)}, s32[16,256]{1,0:T(8,128)S(1)}, /*index=5*/s32[]{:T(128)}, bf16[4,64,8,1024]{1,2,3,0:T(8,128)(2,1)}, ...), branch_computations={%region_1.1_spmd, %region_2.2_spmd} | conditional | flops 312674400 | bytes 23090232 | solution.py:140
  129.7 3.7 %copy.9 = bf16[16,16,512]{1,0,2:T(8,128)(2,1)} copy(bf16[16,16,512]{2,1,0:T(8,128)(2,1)} %get-tuple-element.286) | data formatting | bytes 524288 | tf_op jit(solution)/shard_map/while/body/eval_jaxpr/cond/branch_1_fun/concatenate | solution.py:69
  133.4 4.2 %convert_bitcast_fusion.1 = bf16[16,64,512]{1,0,2:T(8,128)(2,1)} fusion(bf16[16,16,512]{1,0,2:T(8,128)(2,1)} %copy.9, bf16[64,8,512]{0,1,2:T(8,128)(2,1)S(1)} %get-tuple-element.281, bf16[64,8,512]{0,1,2:T(8,128)(2,1)S(1)} %get-tuple-element.282), kind=kOutput, calls=%fused_computation.14 | convolution fusion | flops 19398656 | bytes 2359296 | tf_op jit(solution)/shard_map/while/body/eval_jaxpr/cond/branch_1_fun/asf,bsf->abf/dot_general | solution.py:73
  137.5 3.3 %copy.10 = bf16[16,64,512]{2,1,0:T(8,128)(2,1)} copy(bf16[16,64,512]{1,0,2:T(8,128)(2,1)} %convert_bitcast_fusion.1) | data formatting | bytes 2097152 | tf_op jit(solution)/shard_map/while/body/eval_jaxpr/cond/branch_1_fun/asf,bsf->abf/transpose | solution.py:73
  140.9 2.8 copy.11
  143.7 4.2 %convert_bitcast_fusion = bf16[16,64,512]{1,0,2:T(8,128)(2,1)} fusion(bf16[16,16,512]{1,0,2:T(8,128)(2,1)} %copy.11, bf16[64,8,512]{0,1,2:T(8,128)(2,1)S(1)} %get-tuple-element.282, bf16[64,8,512]{0,1,2:T(8,128)(2,1)S(1)} %get-tuple-element.281), kind=kOutput, calls=%fused_computation.13 | convolution fusion | flops 19398656 | bytes 2359296 | tf_op jit(solution)/shard_map/while/body/eval_jaxpr/cond/branch_1_fun/asf,bsf->abf/dot_general | solution.py:75
  152.9 26.9 %conditional.3 = (f32[128,1024]{1,0:T(8,128)}) conditional(s32[]{:T(128)} %convert_element_type.47, f32[128,1024]{1,0:T(8,128)} %get-tuple-element.346, (s32[]{:T(128)}, s32[1,64]{1,0:T(1,128)S(1)}, s32[]{:T(128)}, s32[16]{0:T(128)S(1)}, s32[16,256]{1,0:T(8,128)S(1)}, /*index=5*/s32[]{:T(128)}, bf16[4,64,8,1024]{1,2,3,0:T(8,128)(2,1)}, ...), branch_computations={%region_1.1_spmd, %region_2.2_spmd} | conditional | flops 312674400 | bytes 23090232 | solution.py:140
  156.6 3.7 %copy.9 = bf16[16,16,512]{1,0,2:T(8,128)(2,1)} copy(bf16[16,16,512]{2,1,0:T(8,128)(2,1)} %get-tuple-element.286) | data formatting | bytes 524288 | tf_op jit(solution)/shard_map/while/body/eval_jaxpr/cond/branch_1_fun/concatenate | solution.py:69
  160.2 4.2 %convert_bitcast_fusion.1 = bf16[16,64,512]{1,0,2:T(8,128)(2,1)} fusion(bf16[16,16,512]{1,0,2:T(8,128)(2,1)} %copy.9, bf16[64,8,512]{0,1,2:T(8,128)(2,1)S(1)} %get-tuple-element.281, bf16[64,8,512]{0,1,2:T(8,128)(2,1)S(1)} %get-tuple-element.282), kind=kOutput, calls=%fused_computation.14 | convolution fusion | flops 19398656 | bytes 2359296 | tf_op jit(solution)/shard_map/while/body/eval_jaxpr/cond/branch_1_fun/asf,bsf->abf/dot_general | solution.py:73
  164.4 3.3 %copy.10 = bf16[16,64,512]{2,1,0:T(8,128)(2,1)} copy(bf16[16,64,512]{1,0,2:T(8,128)(2,1)} %convert_bitcast_fusion.1) | data formatting | bytes 2097152 | tf_op jit(solution)/shard_map/while/body/eval_jaxpr/cond/branch_1_fun/asf,bsf->abf/transpose | solution.py:73
  170.5 4.2 %convert_bitcast_fusion = bf16[16,64,512]{1,0,2:T(8,128)(2,1)} fusion(bf16[16,16,512]{1,0,2:T(8,128)(2,1)} %copy.11, bf16[64,8,512]{0,1,2:T(8,128)(2,1)S(1)} %get-tuple-element.282, bf16[64,8,512]{0,1,2:T(8,128)(2,1)S(1)} %get-tuple-element.281), kind=kOutput, calls=%fused_computation.13 | convolution fusion | flops 19398656 | bytes 2359296 | tf_op jit(solution)/shard_map/while/body/eval_jaxpr/cond/branch_1_fun/asf,bsf->abf/dot_general | solution.py:75
  179.8 26.9 %conditional.3 = (f32[128,1024]{1,0:T(8,128)}) conditional(s32[]{:T(128)} %convert_element_type.47, f32[128,1024]{1,0:T(8,128)} %get-tuple-element.346, (s32[]{:T(128)}, s32[1,64]{1,0:T(1,128)S(1)}, s32[]{:T(128)}, s32[16]{0:T(128)S(1)}, s32[16,256]{1,0:T(8,128)S(1)}, /*index=5*/s32[]{:T(128)}, bf16[4,64,8,1024]{1,2,3,0:T(8,128)(2,1)}, ...), branch_computations={%region_1.1_spmd, %region_2.2_spmd} | conditional | flops 312674400 | bytes 23090232 | solution.py:140
  183.4 3.7 %copy.9 = bf16[16,16,512]{1,0,2:T(8,128)(2,1)} copy(bf16[16,16,512]{2,1,0:T(8,128)(2,1)} %get-tuple-element.286) | data formatting | bytes 524288 | tf_op jit(solution)/shard_map/while/body/eval_jaxpr/cond/branch_1_fun/concatenate | solution.py:69
  187.1 4.2 %convert_bitcast_fusion.1 = bf16[16,64,512]{1,0,2:T(8,128)(2,1)} fusion(bf16[16,16,512]{1,0,2:T(8,128)(2,1)} %copy.9, bf16[64,8,512]{0,1,2:T(8,128)(2,1)S(1)} %get-tuple-element.281, bf16[64,8,512]{0,1,2:T(8,128)(2,1)S(1)} %get-tuple-element.282), kind=kOutput, calls=%fused_computation.14 | convolution fusion | flops 19398656 | bytes 2359296 | tf_op jit(solution)/shard_map/while/body/eval_jaxpr/cond/branch_1_fun/asf,bsf->abf/dot_general | solution.py:73
  191.3 3.3 %copy.10 = bf16[16,64,512]{2,1,0:T(8,128)(2,1)} copy(bf16[16,64,512]{1,0,2:T(8,128)(2,1)} %convert_bitcast_fusion.1) | data formatting | bytes 2097152 | tf_op jit(solution)/shard_map/while/body/eval_jaxpr/cond/branch_1_fun/asf,bsf->abf/transpose | solution.py:73
  194.6 2.8 copy.11
  197.4 4.2 %convert_bitcast_fusion = bf16[16,64,512]{1,0,2:T(8,128)(2,1)} fusion(bf16[16,16,512]{1,0,2:T(8,128)(2,1)} %copy.11, bf16[64,8,512]{0,1,2:T(8,128)(2,1)S(1)} %get-tuple-element.282, bf16[64,8,512]{0,1,2:T(8,128)(2,1)S(1)} %get-tuple-element.281), kind=kOutput, calls=%fused_computation.13 | convolution fusion | flops 19398656 | bytes 2359296 | tf_op jit(solution)/shard_map/while/body/eval_jaxpr/cond/branch_1_fun/asf,bsf->abf/dot_general | solution.py:75
  206.7 26.9 %conditional.3 = (f32[128,1024]{1,0:T(8,128)}) conditional(s32[]{:T(128)} %convert_element_type.47, f32[128,1024]{1,0:T(8,128)} %get-tuple-element.346, (s32[]{:T(128)}, s32[1,64]{1,0:T(1,128)S(1)}, s32[]{:T(128)}, s32[16]{0:T(128)S(1)}, s32[16,256]{1,0:T(8,128)S(1)}, /*index=5*/s32[]{:T(128)}, bf16[4,64,8,1024]{1,2,3,0:T(8,128)(2,1)}, ...), branch_computations={%region_1.1_spmd, %region_2.2_spmd} | conditional | flops 312674400 | bytes 23090232 | solution.py:140
  210.3 3.7 %copy.9 = bf16[16,16,512]{1,0,2:T(8,128)(2,1)} copy(bf16[16,16,512]{2,1,0:T(8,128)(2,1)} %get-tuple-element.286) | data formatting | bytes 524288 | tf_op jit(solution)/shard_map/while/body/eval_jaxpr/cond/branch_1_fun/concatenate | solution.py:69
  214.0 4.2 %convert_bitcast_fusion.1 = bf16[16,64,512]{1,0,2:T(8,128)(2,1)} fusion(bf16[16,16,512]{1,0,2:T(8,128)(2,1)} %copy.9, bf16[64,8,512]{0,1,2:T(8,128)(2,1)S(1)} %get-tuple-element.281, bf16[64,8,512]{0,1,2:T(8,128)(2,1)S(1)} %get-tuple-element.282), kind=kOutput, calls=%fused_computation.14 | convolution fusion | flops 19398656 | bytes 2359296 | tf_op jit(solution)/shard_map/while/body/eval_jaxpr/cond/branch_1_fun/asf,bsf->abf/dot_general | solution.py:73
  218.1 3.3 %copy.10 = bf16[16,64,512]{2,1,0:T(8,128)(2,1)} copy(bf16[16,64,512]{1,0,2:T(8,128)(2,1)} %convert_bitcast_fusion.1) | data formatting | bytes 2097152 | tf_op jit(solution)/shard_map/while/body/eval_jaxpr/cond/branch_1_fun/asf,bsf->abf/transpose | solution.py:73
  221.5 2.8 copy.11
  224.3 4.2 %convert_bitcast_fusion = bf16[16,64,512]{1,0,2:T(8,128)(2,1)} fusion(bf16[16,16,512]{1,0,2:T(8,128)(2,1)} %copy.11, bf16[64,8,512]{0,1,2:T(8,128)(2,1)S(1)} %get-tuple-element.282, bf16[64,8,512]{0,1,2:T(8,128)(2,1)S(1)} %get-tuple-element.281), kind=kOutput, calls=%fused_computation.13 | convolution fusion | flops 19398656 | bytes 2359296 | tf_op jit(solution)/shard_map/while/body/eval_jaxpr/cond/branch_1_fun/asf,bsf->abf/dot_general | solution.py:75
  233.6 9.8 %cosine_multiply_fusion = (f32[512,1024]{1,0:T(8,128)S(1)}, f32[512,1024]{1,0:T(8,128)}) fusion(s32[1024]{0:T(1024)S(1)} %iota_add_fusion, s32[512]{0:T(512)S(1)} %iota_add_fusion.2, f32[512]{0:T(512)S(1)} %get-tuple-element.296, f32[512]{0:T(512)S(1)} %get-tuple-element.297), kind=kLoop, calls=%fused_computation.55 | loop fusion | flops 8388608 | bytes 4204544 | tf_op jit(solution)/shard_map/mul | solution.py:44
  243.4 64.2 %reduce-scatter.3.cloned.1.call-done = f32[8,1024]{1,0:T(8,128)} async-done(((f32[128,1024]{1,0:T(8,128)}), f32[8,1024]{1,0:T(8,128)}) %reduce-scatter.3.cloned.1.call-update) | async-done | bytes 32784 | tf_op jit(solution)/shard_map/reduce_scatter | solution.py:149
  307.6 4.3 %fusion.32 = f32[8,1024]{1,0:T(8,128)} fusion(f32[8,1024]{1,0:T(8,128)} %reduce-scatter.3.cloned.1.call-done, f32[512,1024]{1,0:T(8,128)} %get-tuple-element.293, f32[512,1024]{1,0:T(8,128)S(1)} %get-tuple-element.292), kind=kOutput, calls=%fused_computation.38 | convolution fusion | flops 101711872 | bytes 4259840 | tf_op jit(solution)/shard_map/dot_general | solution.py:150
  311.9 3.9 %reduce-scatter.5.cloned.1.call-done = f32[8,512]{1,0:T(8,128)} async-done(((f32[8,1024]{1,0:T(8,128)}), f32[8,512]{1,0:T(8,128)}) %reduce-scatter.5.cloned.1.call-update) | async-done | bytes 16400 | tf_op jit(solution)/shard_map/reduce_scatter | solution.py:153
  (80 shorter events, 45.6 us)
Async XLA Ops:
  6.5 16.7 %copy-start = (f32[16,8,2048]{2,1,0:T(8,128)S(1)}, f32[16,8,2048]{2,1,0:T(8,128)}, u32[]{:S(2)}) copy-start(f32[16,8,2048]{2,1,0:T(8,128)} %param.6) | copy-start | bytes 3145732
  6.5 106.8 %all-gather.2.cloned.1.call-start = ((), (), s32[]{:S(2)}) async-start(), calls=%async_computation.2 | async-start | bytes 4456448 | tf_op jit(solution)/shard_map/all_gather | solution.py:122
  28.1 3.7 %collective-permute-start = (f32[16,8,32]{2,1,0:T(8,128)S(1)}, f32[16,8,32]{2,1,0:T(8,128)S(1)}, u32[]{:S(2)}, u32[]{:S(2)}) collective-permute-start(f32[16,8,32]{2,1,0:T(8,128)S(1)} %get-tuple-element.290), channel_id=1, source_target_pairs={{0,1},{2,3},{4,5},{6,7},{8,9},{10,11},{12,13},{14,15},{16,17},{18,... | collective-permute-start | bytes 49160 | tf_op jit(solution)/shard_map/ppermute | solution.py:22
  30.5 3.1 collective-permute-start.1
  35.0 272.5 %reduce-scatter.3.cloned.1.call-start = ((), (), s32[]{:S(2)}) async-start(), calls=%async_computation.3 | async-start | bytes 557056 | tf_op jit(solution)/shard_map/reduce_scatter | solution.py:149
  113.3 12.7 %copy-start.2 = (s32[16,256]{1,0:T(8,128)S(1)}, s32[16,256]{1,0:T(8,128)}, u32[]{:S(2)}) copy-start(s32[16,256]{1,0:T(8,128)} %param.7) | copy-start | bytes 49156
  147.8 2.8 copy-start.1
  174.7 2.8 copy-start.1
  201.6 2.8 copy-start.1
  228.4 2.8 copy-start.1
  233.5 82.3 %reduce-scatter.5.cloned.1.call-start = ((), (), s32[]{:S(2)}) async-start(), calls=%async_computation.4 | async-start | bytes 49152 | tf_op jit(solution)/shard_map/reduce_scatter | solution.py:153
Sparse Core Ops, SparseCore 0:
  35.2 78.1 all-gather.1
  233.7 73.8 reduce-scatter.2
  312.0 3.7 reduce-scatter.4
where the time goes:
time: 324 us; the launch traced here: 322 us
  waiting for transfers between devices  148 us (46%)
  local copies, waits for them, and re-layouts  70.2 us (22%)
  matrix products  52.1 us (16%)
  other arithmetic  34.7 us (11%)
  between operations  13.2 us (4%)
  starting transfers between devices  3.73 us (1%)
    all_gather x1, waiting for transfers between devices, local(): remote = lax.all_gather(whitened, 'grp', axis=0, tiled=True)  78.3 us
    reduce_scatter x1, waiting for transfers between devices, local(): lax.psum_scatter(binned, 'grp', scatter_dimension=0, tiled=True)  64.2 us
    cos x1, other arithmetic, forward_table(): return jnp.concatenate([jnp.cos(phase), -jnp.sin(phase)], axis=1)  16.7 us
    dot_general x4, matrix products, add_block(): jnp.einsum('asf,bsf->abf', own_alt, far_alt, preferred_element_type=jnp.f...  16.6 us
    dot_general x4, matrix products, add_block(): jnp.einsum('asf,bsf->abf', own_stack, far_stack, preferred_element_type=j...  16.6 us
    concatenate x4, local copies, waits for them, and re-layouts, add_block(): own_stack = jnp.concatenate([own_real, own_imag], axis=1)  14.7 us
    transpose x4, local copies, waits for them, and re-layouts, add_block(): jnp.einsum('asf,bsf->abf', own_stack, far_stack, preferred_element_type=j...  13.3 us
    unnamed x5, local copies, waits for them, and re-layouts  11.8 us
  transfers between devices with their start and end apart: 5, of which 4 were waited for; matrix products, arithmetic and copies ran while one was open for 3% of the time, Pallas kernels for 0%

commit v1 on v0

--- a/solution.py
+++ b/solution.py
@@ -2,7 +2,11 @@
 
 import jax
 import jax.numpy as jnp
+import ml_dtypes
+import numpy as np
 from jax import lax
+from jax.experimental import pallas as pl
+from jax.experimental.pallas import tpu as pltpu
 from jax.sharding import PartitionSpec as P
 
 NFFT = 2048
@@ -153,7 +157,336 @@
     return lax.psum_scatter(lag_partial, "lag", scatter_dimension=1, tiled=True)
 
 
+LANES = 128
+RADIX = 4
+SPLIT = NFFT // RADIX
+PACK = 16
+
+
+def halves(table):
+    wide = np.asarray(table, np.float32)
+    high = wide.astype(ml_dtypes.bfloat16)
+    return high, (wide - high.astype(np.float32)).astype(ml_dtypes.bfloat16)
+
+
+def forward_constants(freq_count, lag_count):
+    high, low, halo, band, inverse_count = [], [], [], [], []
+    sample = np.arange(SPLIT)
+    for index in range(lag_count):
+        start = index * freq_count
+        order = start + np.concatenate(
+            [np.arange(freq_count // RADIX) * RADIX + r for r in range(RADIX)]
+        )
+        per_class = order.reshape(RADIX, -1)
+        angle = 2.0 * np.pi / NFFT * (sample[None, :, None] * per_class[:, None, :] % NFFT)
+        table = np.concatenate([np.cos(angle), np.sin(angle)], axis=2)
+        table_high, table_low = halves(table)
+        high.append(table_high)
+        low.append(table_low)
+        beyond = np.concatenate(
+            [np.arange(start - HW, start), np.arange(start + freq_count, start + freq_count + HW)]
+        )
+        beyond = beyond[(beyond >= 0) & (beyond < NFFT // 2)]
+        angle = 2.0 * np.pi / NFFT * (np.arange(NFFT)[:, None] * beyond[None, :] % NFFT)
+        side = np.zeros((NFFT, 2 * LANES))
+        side[:, : beyond.size] = np.cos(angle)
+        side[:, LANES : LANES + beyond.size] = np.sin(angle)
+        halo.append(halves(side)[0])
+        near = np.zeros((freq_count + LANES, freq_count))
+        seen = np.concatenate([order, beyond])
+        near[: seen.size] = np.abs(seen[:, None] - order[None, :]) <= HW
+        band.append(near.astype(ml_dtypes.bfloat16))
+        upper = np.minimum(order + HW, NFFT // 2 - 1)
+        lower = np.maximum(order - HW, 0)
+        inverse_count.append((1.0 / (upper - lower + 1))[None, :].astype(np.float32))
+    return tuple(np.stack(part) for part in (high, low, halo, band, inverse_count))
+
+
+def inverse_constants(freq_count, lag_count, groups):
+    run = freq_count // groups
+    quarter = run // RADIX
+    index = np.arange(groups * lag_count)
+    start = (index % lag_count) * freq_count + (index // lag_count) * run
+    pair, half, step = np.meshgrid(np.arange(2), np.arange(2), np.arange(quarter), indexing="ij")
+    offset = (RADIX * step + 2 * pair + half).reshape(2, PACK)
+    bins = start[:, None, None] + offset[None]
+    both = np.stack([bins, bins], axis=2)
+    imaginary = np.stack([np.zeros_like(bins), np.ones_like(bins)], axis=2).reshape(-1)
+    both = both.reshape(-1)
+    angle = 2.0 * np.pi / NFFT * (both[:, None] * np.arange(LANES)[None, :] % NFFT)
+    table = np.where(imaginary[:, None] == 1, -np.sin(angle), np.cos(angle))
+    table_high, table_low = halves(table)
+    lag_block = LAGS // lag_count
+    weight = np.where(both == 0, 1.0, 2.0) / NFFT
+    own, swapped = [], []
+    for lag in range(lag_count):
+        first = np.arange(lag_block // LANES) * LANES + lag * lag_block - LAGS // 2
+        angle = 2.0 * np.pi / NFFT * (both[None, :] * first[:, None] % NFFT)
+        own.append(weight * np.cos(angle))
+        swapped.append(np.where(imaginary == 1, 1.0, -1.0) * weight * np.sin(angle))
+    return (
+        table_high,
+        table_low,
+        np.stack(own).astype(np.float32),
+        np.stack(swapped).astype(np.float32),
+    )
+
+
+def split_float(value):
+    high = value.astype(jnp.bfloat16)
+    return high, (value - high.astype(jnp.float32)).astype(jnp.bfloat16)
+
+
+def product(left, right):
+    return jnp.dot(left, right, preferred_element_type=jnp.float32)
+
+
+def product_transposed(left, right):
+    return lax.dot_general(
+        left, right, (((1,), (1,)), ((), ())), preferred_element_type=jnp.float32
+    )
+
+
+def whiten_kernel(
+    lag_ref, wave_ref, bin_ref, high_ref, low_ref, halo_ref, band_ref, count_ref, out_ref, scratch
+):
+    rows = wave_ref.shape[0]
+    segments = rows // PACK
+    targets = out_ref.shape[0]
+    wave = wave_ref[...]
+    quarter = [wave[:, k * SPLIT : (k + 1) * SPLIT] for k in range(RADIX)]
+    even_sum = quarter[0] + quarter[2]
+    odd_sum = quarter[1] + quarter[3]
+    even_high, even_low = split_float(quarter[0] - quarter[2])
+    odd_high, odd_low = split_float(quarter[1] - quarter[3])
+    real, imag = [None] * RADIX, [None] * RADIX
+    for r, folded in ((0, even_sum + odd_sum), (2, even_sum - odd_sum)):
+        folded_high, folded_low = split_float(folded)
+        value = product(folded_high, high_ref[r]) + product(folded_low, high_ref[r])
+        value = value + product(folded_high, low_ref[r])
+        real[r] = value[:, :LANES]
+        imag[r] = -value[:, LANES:]
+    stacked_high = jnp.concatenate([even_high, odd_high], axis=0)
+    stacked_low = jnp.concatenate([even_low, odd_low], axis=0)
+    for r, sign in ((1, 1.0), (3, -1.0)):
+        value = product(stacked_high, high_ref[r]) + product(stacked_low, high_ref[r])
+        value = value + product(stacked_high, low_ref[r])
+        real[r] = value[:rows, :LANES] - sign * value[rows:, LANES:]
+        imag[r] = -value[:rows, LANES:] - sign * value[rows:, :LANES]
+    beyond = product(wave.astype(jnp.bfloat16), halo_ref[...])
+    parts = [jnp.sqrt(real[r] * real[r] + imag[r] * imag[r]) for r in range(RADIX)]
+    side_real, side_imag = beyond[:, :LANES], beyond[:, LANES:]
+    parts.append(jnp.sqrt(side_real * side_real + side_imag * side_imag))
+    amplitude_high, amplitude_low = split_float(jnp.concatenate(parts, axis=1))
+    total = product(amplitude_high, band_ref[...]) + product(amplitude_low, band_ref[...])
+    inverse = 1.0 / (total * count_ref[...] + EPSILON)
+    for r in range(RADIX):
+        scale = inverse[:, r * LANES : (r + 1) * LANES]
+        scratch[0, r] = real[r] * scale
+        scratch[1, r] = imag[r] * scale
+    width = LANES // targets
+    chunk = lax.broadcasted_iota(jnp.int32, (PACK, LANES), 1) // width
+    for pair in range(2):
+        for part in range(2):
+            rolled = []
+            for half in range(2):
+                for segment in range(segments):
+                    rows_of = scratch[part, 2 * pair + half, pl.ds(segment, PACK, stride=segments), :]
+                    shift = width * (half * segments + segment)
+                    rolled.append(pltpu.roll(rows_of, shift, 1) if shift else rows_of)
+            for target in range(targets):
+                value = rolled[-target % targets]
+                for place in range(1, targets):
+                    value = jnp.where(chunk == place, rolled[(place - target) % targets], value)
+                out_ref[target, 2 * pair + part] = value.astype(jnp.bfloat16)
+    bins = bin_ref[...].astype(jnp.float32).astype(jnp.bfloat16)
+    for target in range(targets):
+        for k in range(bins.shape[1] // LANES):
+            out_ref[target, 4 + k] = bins[:, k * LANES : (k + 1) * LANES]
+
+
+def pair_kernel(group_ref, data_ref, out_ref, spectra, bins, cross, total):
+    groups = data_ref.shape[0]
+    stations = groups * PACK
+    bin_count = total.shape[1]
+    width = LANES // groups
+    for group in range(groups):
+        rows = pl.ds(group * PACK, PACK)
+        for pair in range(2):
+            for part in range(2):
+                spectra[pair, rows, part * LANES : (part + 1) * LANES] = data_ref[
+                    group, 2 * pair + part
+                ]
+        for k in range(stations // LANES):
+            bins[rows, k * LANES : (k + 1) * LANES] = data_ref[group, 4 + k]
+    total[...] = jnp.zeros_like(total)
+    lane = lax.broadcasted_iota(jnp.int32, (PACK, 2 * LANES), 1) % LANES
+    place = (lane // width - group_ref[0] + groups) % groups
+    slot = place // (groups // 2) * width + lane % width
+    row = lax.broadcasted_iota(jnp.int32, (PACK, 2 * LANES), 0)
+    keep = (slot == row).astype(jnp.float32)[None]
+
+    def one_group(group, first_column):
+        start = pl.multiple_of(group * PACK, PACK)
+        columns = stations - first_column
+        for pair in range(2):
+            own = spectra[pair, pl.ds(start, PACK), :].astype(jnp.float32)
+            turned = jnp.concatenate([-own[:, LANES:], own[:, :LANES]], axis=1)
+            diagonal = jnp.concatenate(
+                [own[:, None, :] * keep, turned[:, None, :] * keep], axis=1
+            ).astype(jnp.bfloat16)
+            value = product_transposed(
+                diagonal.reshape(PACK * 2 * PACK, 2 * LANES), spectra[pair, first_column:, :]
+            )
+            cross[:, pair * 2 * PACK : (pair + 1) * 2 * PACK, first_column:] = value.astype(
+                jnp.bfloat16
+            ).reshape(PACK, 2 * PACK, columns)
+        column = first_column + lax.broadcasted_iota(jnp.int32, (PACK, columns), 1)
+        station = start + lax.broadcasted_iota(jnp.int32, (PACK, columns), 0)
+        own_bins = bins[pl.ds(start, PACK), first_column:].astype(jnp.float32)
+        own_bins = jnp.where(column > station, own_bins, -1.0)
+        wanted = lax.broadcasted_iota(jnp.int32, (bin_count, columns), 0).astype(jnp.float32)
+        value = total[...]
+        for i in range(PACK):
+            onehot = (own_bins[i : i + 1, :] == wanted).astype(jnp.float32).astype(jnp.bfloat16)
+            value = value + product_transposed(cross[i, :, first_column:], onehot)
+        total[...] = value
+
+    for block in range(stations // LANES):
+        per_block = LANES // PACK
+
+        def body(group, carry, first_column=block * LANES):
+            one_group(group, first_column)
+            return carry
+
+        lax.fori_loop(block * per_block, (block + 1) * per_block, body, 0)
+    out_ref[...] = total[...].T
+
+
+def lag_kernel(lag_ref, data_ref, high_ref, low_ref, own_ref, swapped_ref, out_ref):
+    sources, owned, width = data_ref.shape
+    lane = lax.broadcasted_iota(jnp.int32, (owned, LANES), 1)
+    is_real = lane % (2 * PACK) < PACK
+    per_tile = LANES // width
+    blocks = out_ref.shape[1] // LANES
+    turned = [[] for _ in range(blocks)]
+    for tile in range(sources // per_tile):
+        value = jnp.concatenate(
+            [data_ref[tile * per_tile + k] for k in range(per_tile)], axis=1
+        )
+        partner = jnp.where(
+            is_real, pltpu.roll(value, LANES - PACK, 1), pltpu.roll(value, PACK, 1)
+        )
+        at = slice(tile * LANES, (tile + 1) * LANES)
+        for block in range(blocks):
+            turned[block].append(
+                value * own_ref[block : block + 1, at] + partner * swapped_ref[block : block + 1, at]
+            )
+    left = jnp.concatenate([jnp.concatenate(row, axis=1) for row in turned], axis=0)
+    left_high, left_low = split_float(left)
+    value = product(left_high, high_ref[...]) + product(left_low, high_ref[...])
+    value = value + product(left_high, low_ref[...])
+    for block in range(blocks):
+        out_ref[:, block * LANES : (block + 1) * LANES] = value[block * owned : (block + 1) * owned]
+
+
+def whole_block(array):
+    return pl.BlockSpec(array.shape, lambda i, s: (0,) * array.ndim)
+
+
+def lag_part(array):
+    return pl.BlockSpec(
+        (None,) + array.shape[1:], lambda i, s: (s[0],) + (0,) * (array.ndim - 1)
+    )
+
+
+def call(kernel, scalar, arrays, specs, out_shape, scratch=()):
+    grid_spec = pltpu.PrefetchScalarGridSpec(
+        num_scalar_prefetch=1,
+        grid=(1,),
+        in_specs=specs,
+        out_specs=whole_block(out_shape),
+        scratch_shapes=list(scratch),
+    )
+    return pl.pallas_call(
+        kernel,
+        grid_spec=grid_spec,
+        out_shape=out_shape,
+        compiler_params=pltpu.CompilerParams(vmem_limit_bytes=48 << 20),
+    )(scalar, *arrays)
+
+
+def local_by_frequency(waveforms, pair_bin):
+    station_count, segments, _ = waveforms.shape
+    groups = lax.axis_size("grp")
+    lag_count = lax.axis_size("lag")
+    freq_count = NFFT // 2 // lag_count
+    stations = station_count * groups
+    bin_count = BIN_DEV * groups
+    lag_index = lax.axis_index("lag").astype(jnp.int32).reshape(1)
+    group_index = lax.axis_index("grp").astype(jnp.int32).reshape(1)
+    rows = waveforms.reshape(station_count * segments, NFFT)
+    tables = [jnp.asarray(t) for t in forward_constants(freq_count, lag_count)]
+    blocks = 4 + stations // LANES
+    whitened = call(
+        whiten_kernel,
+        lag_index,
+        [rows, pair_bin, *tables],
+        [whole_block(rows), whole_block(pair_bin), *[lag_part(t) for t in tables]],
+        jax.ShapeDtypeStruct((groups, blocks, PACK, LANES), jnp.bfloat16),
+        [pltpu.VMEM((2, RADIX, station_count * segments, LANES), jnp.float32)],
+    )
+    received = lax.all_to_all(whitened, "grp", 0, 0, tiled=True)
+    binned = call(
+        pair_kernel,
+        group_index,
+        [received],
+        [whole_block(received)],
+        jax.ShapeDtypeStruct((bin_count, 4 * PACK), jnp.float32),
+        [
+            pltpu.VMEM((2, stations, 2 * LANES), jnp.bfloat16),
+            pltpu.VMEM((stations, stations), jnp.bfloat16),
+            pltpu.VMEM((PACK, 4 * PACK, stations), jnp.bfloat16),
+            pltpu.VMEM((4 * PACK, bin_count), jnp.float32),
+        ],
+    )
+    outgoing = jnp.broadcast_to(
+        binned.reshape(groups, 1, BIN_DEV, 4 * PACK), (groups, lag_count, BIN_DEV, 4 * PACK)
+    ).reshape(groups * lag_count, BIN_DEV, 4 * PACK)
+    owned = lax.all_to_all(outgoing, ("grp", "lag"), 0, 0, tiled=True)
+    high, low, own, swapped = [
+        jnp.asarray(t) for t in inverse_constants(freq_count, lag_count, groups)
+    ]
+    return call(
+        lag_kernel,
+        lag_index,
+        [owned, high, low, own, swapped],
+        [whole_block(owned), whole_block(high), whole_block(low), lag_part(own), lag_part(swapped)],
+        jax.ShapeDtypeStruct((BIN_DEV, LAGS // lag_count), jnp.float32),
+    )
+
+
+def fits_by_frequency(mesh, waveforms):
+    groups, lag_count = mesh.shape["grp"], mesh.shape["lag"]
+    stations, segments, _ = waveforms.shape
+    freq_count = NFFT // 2 // lag_count
+    return (
+        lag_count == 2
+        and stations == groups * PACK
+        and freq_count == RADIX * LANES
+        and segments * 2 * (LANES // groups) == LANES
+        and groups * BIN_DEV <= 256
+    )
+
+
 def solution(mesh):
     in_specs = (P("grp", None, None), P("grp", None))
     out_specs = P("grp", "lag")
-    return jax.shard_map(local, mesh=mesh, in_specs=in_specs, out_specs=out_specs, check_vma=False)
+
+    def run(waveforms, pair_bin):
+        body = local_by_frequency if fits_by_frequency(mesh, waveforms) else local
+        return jax.shard_map(
+            body, mesh=mesh, in_specs=in_specs, out_specs=out_specs, check_vma=False
+        )(waveforms, pair_bin)
+
+    return run

time: 324 us -> 57.5 us (0.18)
  waiting for transfers between devices: 148 us -> 12.6 us
  local copies, waits for them, and re-layouts: 70.2 us -> 6.28 us
  matrix products: 52.1 us -> 0 us
  other arithmetic: 34.7 us -> 0.8 us
  Pallas kernels: 0 us -> 19 us
  between operations: 13.2 us -> 0.09 us
  blocking collectives: 0 us -> 9.78 us
  starting transfers between devices: 3.73 us -> 8.46 us
    all_gather x1 -> x0, waiting for transfers between devices: 78.3 us -> none  [local(): remote = lax.all_gather(whitened, 'grp', axis=0, tiled=True)]
    reduce_scatter x2 -> x0, waiting for transfers between devices: 68.1 us -> none  [the longest x1 64.2 us: local(): lax.psum_scatter(binned, 'grp', scatter_dimension=0, tiled=True)]
    dot_general x15 -> x0, matrix products: 52.1 us -> none  [the longest x4 16.6 us: add_block(): jnp.einsum('asf,bsf->abf', own_alt, far_alt, preferred_element_type=jnp.f...]
    concatenate x8 -> x0, local copies, waits for them, and re-layouts: 25.9 us -> none  [the longest x4 14.7 us: add_block(): own_stack = jnp.concatenate([own_real, own_imag], axis=1)]
    transpose x8 -> x0, local copies, waits for them, and re-layouts: 23.7 us -> none  [the longest x4 13.3 us: add_block(): jnp.einsum('asf,bsf->abf', own_stack, far_stack, preferred_element_type=j...]
    pallas_call x0 -> x3, Pallas kernels: none -> 19 us  [call(): pl.pallas_call(kernel, grid_spec=grid_spec, out_shape=out_shape, compiler...]
    cos x1 -> x0, other arithmetic: 16.7 us -> none  [forward_table(): return jnp.concatenate([jnp.cos(phase), -jnp.sin(phase)], axis=1)]
    all_to_all x0 -> x1, waiting for transfers between devices: none -> 12.6 us  [local_by_frequency(): received = lax.all_to_all(whitened, 'grp', 0, 0, tiled=True)]
  transfers between devices with their start and end apart: 5 -> 1, of which waited for: 4 -> 1; matrix products, arithmetic and copies ran while one was open for 3% -> 0% of each run, Pallas kernels for 0% -> 0%
where the time goes in v1:
time: 57.5 us; the launch traced here: 57.1 us
  Pallas kernels  19 us (33%)
  waiting for transfers between devices  12.6 us (22%)
  blocking collectives  9.78 us (17%)
  starting transfers between devices  8.46 us (15%)
  local copies, waits for them, and re-layouts  6.28 us (11%)
  other arithmetic  0.8 us (1%)
    pallas_call x3, Pallas kernels, call(): pl.pallas_call(kernel, grid_spec=grid_spec, out_shape=out_shape, compiler...  19 us
    all_to_all x1, waiting for transfers between devices, local_by_frequency(): received = lax.all_to_all(whitened, 'grp', 0, 0, tiled=True)  12.6 us
    all_to_all x1, blocking collectives, local_by_frequency(): owned = lax.all_to_all(outgoing, ('grp', 'lag'), 0, 0, tiled=True)  9.78 us
    all_to_all x1, starting transfers between devices, local_by_frequency(): received = lax.all_to_all(whitened, 'grp', 0, 0, tiled=True)  8.46 us
    unnamed x20, local copies, waits for them, and re-layouts  5.76 us
  transfers between devices with their start and end apart: 1, of which 1 were waited for; matrix products, arithmetic and copies ran while one was open for 0% of the time, Pallas kernels for 0%

profile of v1, /device:TPU:0, one launch (start us, length us, event | category | flops | bytes accessed | tf_op | source)
XLA Modules:
  0.0 57.1 jit_solution(9689778005000708486)
XLA Ops:
  0.0 0.0 copy-start
  0.0 1.6 %copy-done = bf16[2,4,512,256]{3,2,1,0:T(8,128)(2,1)S(1)} copy-done((bf16[2,4,512,256]{3,2,1,0:T(8,128)(2,1)S(1)}, bf16[2,4,512,256]{3,2,1,0:T(8,128)(2,1)}, u32[]{:S(2)}) %copy-start) | copy-done | bytes 2097176
  1.6 0.0 copy-start.1
  1.6 1.3 %copy-done.1 = bf16[2,640,512]{2,1,0:T(8,128)(2,1)S(1)} copy-done((bf16[2,640,512]{2,1,0:T(8,128)(2,1)S(1)}, bf16[2,640,512]{2,1,0:T(8,128)(2,1)}, u32[]{:S(2)}) %copy-start.1) | copy-done | bytes 1310744
  2.9 0.0 copy-start.2
  2.9 1.2 %copy-done.2 = f32[16,8,2048]{2,1,0:T(8,128)S(1)} copy-done((f32[16,8,2048]{2,1,0:T(8,128)S(1)}, f32[16,8,2048]{2,1,0:T(8,128)}, u32[]{:S(2)}) %copy-start.2) | copy-done | bytes 1048600
  4.1 0.0 copy-start.7
  4.1 0.7 %copy-done.7 = s32[16,256]{1,0:T(8,128)S(1)} copy-done((s32[16,256]{1,0:T(8,128)S(1)}, s32[16,256]{1,0:T(8,128)}, u32[]{:S(2)}) %copy-start.7) | copy-done | bytes 16408
  4.9 0.0 copy-start.8
  4.9 0.7 %copy-done.8 = f32[2,1,512]{2,1,0:T(1,128)S(1)} copy-done((f32[2,1,512]{2,1,0:T(1,128)S(1)}, f32[2,1,512]{2,1,0:T(1,128)}, u32[]{:S(2)}) %copy-start.8) | copy-done | bytes 4120
  5.5 4.2 %shard_map.109 = bf16[16,6,16,128]{3,2,1,0:T(8,128)(2,1)} custom-call(s32[1]{0:T(128)} %bitcast.lag_ref, f32[128,2048]{1,0:T(8,128)S(1)} %bitcast.5, s32[16,256]{1,0:T(8,128)S(1)} %copy-done.7, bf16[2,4,512,256]{3,2,1,0:T(8,128)(2,1)S(1)} %copy-done, bf16[2,4,512,256]{3,2,1,0:T(8,128)(2,1)} %constant.27.clone.low_ref, ...), custom_call_target="tpu_custom_call" | custom-call | tf_op jit(solution)/shard_map/pallas_call | solution.py:411
  9.8 0.0 copy-start.3
  9.8 0.0 copy-start.4
  9.8 0.0 copy-start.5
  9.8 0.0 copy-start.6
  9.8 8.5 %all-to-all-start = ((bf16[16,6,16,128]{3,2,1,0:T(8,128)(2,1)}), bf16[16,6,16,128]{3,2,1,0:T(8,128)(2,1)S(1)}, u32[]{:S(2)}, u32[]{:S(2)}) async-start(bf16[16,6,16,128]{3,2,1,0:T(8,128)(2,1)} %shard_map.109), calls=%async_computation | async-start | bytes 786432 | tf_op jit(solution)/shard_map/all_to_all | solution.py:439
  18.3 12.6 %all-to-all-done.data_ref = bf16[16,6,16,128]{3,2,1,0:T(8,128)(2,1)S(1)} async-done(((bf16[16,6,16,128]{3,2,1,0:T(8,128)(2,1)}), bf16[16,6,16,128]{3,2,1,0:T(8,128)(2,1)S(1)}, u32[]{:S(2)}, u32[]{:S(2)}) %all-to-all-start) | async-done | bytes 393248 | tf_op jit(solution)/shard_map/all_to_all | solution.py:439
  30.9 13.7 %shard_map.110 = f32[128,64]{1,0:T(8,128)S(1)} custom-call(s32[1]{0:T(128)} %bitcast.1.group_ref, bf16[16,6,16,128]{3,2,1,0:T(8,128)(2,1)S(1)} %all-to-all-done.data_ref), custom_call_target="tpu_custom_call" | custom-call | tf_op jit(solution)/shard_map/pallas_call | solution.py:411
  44.6 0.1 reshape.18
  44.7 9.8 %all_to_all.10 = f32[32,1,512]{2,1,0:T(1,128)S(1)} all-to-all(f32[32,1,512]{2,1,0:T(1,128)S(1)} %reshape.18), channel_id=1, replica_groups=mesh['grp'=16,'lag'=2] {'grp','lag'}, dimensions={0} | all-to-all | bytes 131072 | tf_op jit(solution)/shard_map/all_to_all | solution.py:456
  54.5 0.5 broadcast
  55.0 0.8 %reduce = f32[32,512]{1,0:T(8,128)S(1)} reduce(f32[32,1,512]{2,1,0:T(1,128)S(1)} %all_to_all.10, f32[]{:T(128)} %broadcast), dimensions={1}, to_apply=%all_to_all.7.reduce_sub_computation | reduce | bytes 131076 | tf_op jit(solution)/shard_map/all_to_all | solution.py:456
  55.8 0.1 reshape.19.data_ref
  55.9 0.0 copy-done.3
  55.9 0.0 copy-done.4
  55.9 0.0 copy-done.5
  55.9 0.0 copy-done.6
  56.0 1.1 %shard_map.111 = f32[8,512]{1,0:T(8,128)} custom-call(s32[1]{0:T(128)} %bitcast.lag_ref, f32[32,8,64]{2,1,0:T(8,128)S(1)} %reshape.19.data_ref, bf16[2048,128]{1,0:T(8,128)(2,1)S(1)} %copy-done.3, bf16[2048,128]{1,0:T(8,128)(2,1)S(1)} %copy-done.4, f32[2,4,2048]{2,1,0:T(4,128)S(1)} %copy-done.5, f32[2,4,2048]{2,1,0:T(4,128)S(1)} %copy-done.6), custom_call_target="tpu_custom_call" | custom-call | tf_op jit(solution)/shard_map/pallas_call | solution.py:411
  (1 shorter events, 0.0 us)
Async XLA Ops:
  0.0 1.6 %copy-start = (bf16[2,4,512,256]{3,2,1,0:T(8,128)(2,1)S(1)}, bf16[2,4,512,256]{3,2,1,0:T(8,128)(2,1)}, u32[]{:S(2)}) copy-start(bf16[2,4,512,256]{3,2,1,0:T(8,128)(2,1)} %constant.26.clone.high_ref) | copy-start | bytes 6291460
  1.6 1.3 %copy-start.1 = (bf16[2,640,512]{2,1,0:T(8,128)(2,1)S(1)}, bf16[2,640,512]{2,1,0:T(8,128)(2,1)}, u32[]{:S(2)}) copy-start(bf16[2,640,512]{2,1,0:T(8,128)(2,1)} %constant.29.clone.band_ref) | copy-start | bytes 3932164
  2.9 1.2 %copy-start.2 = (f32[16,8,2048]{2,1,0:T(8,128)S(1)}, f32[16,8,2048]{2,1,0:T(8,128)}, u32[]{:S(2)}) copy-start(f32[16,8,2048]{2,1,0:T(8,128)} %param.11) | copy-start | bytes 3145732
  4.1 0.7 %copy-start.7 = (s32[16,256]{1,0:T(8,128)S(1)}, s32[16,256]{1,0:T(8,128)}, u32[]{:S(2)}) copy-start(s32[16,256]{1,0:T(8,128)} %bin_ref.1) | copy-start | bytes 49156
  4.9 0.7 %copy-start.8 = (f32[2,1,512]{2,1,0:T(1,128)S(1)}, f32[2,1,512]{2,1,0:T(1,128)}, u32[]{:S(2)}) copy-start(f32[2,1,512]{2,1,0:T(1,128)} %constant.30.clone.count_ref) | copy-start | bytes 12292
  9.8 46.1 %copy-start.3 = (bf16[2048,128]{1,0:T(8,128)(2,1)S(1)}, bf16[2048,128]{1,0:T(8,128)(2,1)}, u32[]{:S(2)}) copy-start(bf16[2048,128]{1,0:T(8,128)(2,1)} %constant.31.clone.high_ref) | copy-start | bytes 1572868
  9.8 46.1 %copy-start.4 = (bf16[2048,128]{1,0:T(8,128)(2,1)S(1)}, bf16[2048,128]{1,0:T(8,128)(2,1)}, u32[]{:S(2)}) copy-start(bf16[2048,128]{1,0:T(8,128)(2,1)} %constant.32.clone.low_ref) | copy-start | bytes 1572868
  9.8 46.2 %copy-start.5 = (f32[2,4,2048]{2,1,0:T(4,128)S(1)}, f32[2,4,2048]{2,1,0:T(4,128)}, u32[]{:S(2)}) copy-start(f32[2,4,2048]{2,1,0:T(4,128)} %constant.33.clone.own_ref) | copy-start | bytes 196612
  9.8 46.2 %copy-start.6 = (f32[2,4,2048]{2,1,0:T(4,128)S(1)}, f32[2,4,2048]{2,1,0:T(4,128)}, u32[]{:S(2)}) copy-start(f32[2,4,2048]{2,1,0:T(4,128)} %constant.34.clone.swapped_ref) | copy-start | bytes 196612
  9.8 21.1 %all-to-all-start = ((bf16[16,6,16,128]{3,2,1,0:T(8,128)(2,1)}), bf16[16,6,16,128]{3,2,1,0:T(8,128)(2,1)S(1)}, u32[]{:S(2)}, u32[]{:S(2)}) async-start(bf16[16,6,16,128]{3,2,1,0:T(8,128)(2,1)} %shard_map.109), calls=%async_computation | async-start | bytes 786432 | tf_op jit(solution)/shard_map/all_to_all | solution.py:439

commit v2 on v1

--- a/solution.py
+++ b/solution.py
@@ -170,36 +170,38 @@
 
 
 def forward_constants(freq_count, lag_count):
-    high, low, halo, band, inverse_count = [], [], [], [], []
+    steps = freq_count // RADIX
     sample = np.arange(SPLIT)
+    width = HW // RADIX
+    beyond = np.stack([steps + np.arange(width), np.arange(width) - width])
+    beyond = beyond.reshape(-1)
+    table = np.zeros((SPLIT, 4 * LANES))
+    angle = 2.0 * np.pi / SPLIT * (sample[:, None] * np.arange(steps)[None, :] % SPLIT)
+    table[:, :steps] = np.cos(angle)
+    table[:, LANES : LANES + steps] = np.sin(angle)
+    angle = 2.0 * np.pi / SPLIT * (sample[:, None] * beyond[None, :] % SPLIT)
+    table[:, 2 * LANES : 2 * LANES + beyond.size] = np.cos(angle)
+    table[:, 3 * LANES : 3 * LANES + beyond.size] = np.sin(angle)
+    high, low = halves(table)
+    tables = np.concatenate([high, low[:, : 2 * LANES]], axis=1)
+    order = np.concatenate([np.arange(steps) * RADIX + r for r in range(RADIX)])
+    outside = np.concatenate([beyond * RADIX + r for r in range(RADIX)])
+    seen = np.concatenate([order, outside])
+    band = np.zeros((freq_count + LANES, freq_count))
+    band[: seen.size] = np.abs(seen[:, None] - order[None, :]) <= HW
+    small = np.zeros((lag_count, 2 * RADIX + 8, freq_count), np.float32)
     for index in range(lag_count):
         start = index * freq_count
-        order = start + np.concatenate(
-            [np.arange(freq_count // RADIX) * RADIX + r for r in range(RADIX)]
-        )
-        per_class = order.reshape(RADIX, -1)
-        angle = 2.0 * np.pi / NFFT * (sample[None, :, None] * per_class[:, None, :] % NFFT)
-        table = np.concatenate([np.cos(angle), np.sin(angle)], axis=2)
-        table_high, table_low = halves(table)
-        high.append(table_high)
-        low.append(table_low)
-        beyond = np.concatenate(
-            [np.arange(start - HW, start), np.arange(start + freq_count, start + freq_count + HW)]
-        )
-        beyond = beyond[(beyond >= 0) & (beyond < NFFT // 2)]
-        angle = 2.0 * np.pi / NFFT * (np.arange(NFFT)[:, None] * beyond[None, :] % NFFT)
-        side = np.zeros((NFFT, 2 * LANES))
-        side[:, : beyond.size] = np.cos(angle)
-        side[:, LANES : LANES + beyond.size] = np.sin(angle)
-        halo.append(halves(side)[0])
-        near = np.zeros((freq_count + LANES, freq_count))
-        seen = np.concatenate([order, beyond])
-        near[: seen.size] = np.abs(seen[:, None] - order[None, :]) <= HW
-        band.append(near.astype(ml_dtypes.bfloat16))
-        upper = np.minimum(order + HW, NFFT // 2 - 1)
-        lower = np.maximum(order - HW, 0)
-        inverse_count.append((1.0 / (upper - lower + 1))[None, :].astype(np.float32))
-    return tuple(np.stack(part) for part in (high, low, halo, band, inverse_count))
+        for r in range(RADIX):
+            angle = 2.0 * np.pi / NFFT * ((start + r) * sample % NFFT)
+            small[index, 2 * r] = np.cos(angle)
+            small[index, 2 * r + 1] = np.sin(angle)
+        upper = np.minimum(start + order + HW, NFFT // 2 - 1)
+        lower = np.maximum(start + order - HW, 0)
+        small[index, 2 * RADIX] = 1.0 / (upper - lower + 1)
+        there = (start + outside >= 0) & (start + outside < NFFT // 2)
+        small[index, 2 * RADIX + 1, : outside.size] = there
+    return small, tables, band.astype(ml_dtypes.bfloat16)
 
 
 def inverse_constants(freq_count, lag_count, groups):
@@ -248,42 +250,86 @@
 
 
 def whiten_kernel(
-    lag_ref, wave_ref, bin_ref, high_ref, low_ref, halo_ref, band_ref, count_ref, out_ref, scratch
+    place_ref, bin_ref, wave_hbm, small_hbm, table_hbm, band_hbm, out_ref,
+    wave_ref, small_ref, table_ref, band_ref, scratch, sems,
 ):
     rows = wave_ref.shape[0]
     segments = rows // PACK
     targets = out_ref.shape[0]
-    wave = wave_ref[...]
-    quarter = [wave[:, k * SPLIT : (k + 1) * SPLIT] for k in range(RADIX)]
-    even_sum = quarter[0] + quarter[2]
-    odd_sum = quarter[1] + quarter[3]
-    even_high, even_low = split_float(quarter[0] - quarter[2])
-    odd_high, odd_low = split_float(quarter[1] - quarter[3])
-    real, imag = [None] * RADIX, [None] * RADIX
-    for r, folded in ((0, even_sum + odd_sum), (2, even_sum - odd_sum)):
-        folded_high, folded_low = split_float(folded)
-        value = product(folded_high, high_ref[r]) + product(folded_low, high_ref[r])
-        value = value + product(folded_high, low_ref[r])
-        real[r] = value[:, :LANES]
-        imag[r] = -value[:, LANES:]
-    stacked_high = jnp.concatenate([even_high, odd_high], axis=0)
-    stacked_low = jnp.concatenate([even_low, odd_low], axis=0)
-    for r, sign in ((1, 1.0), (3, -1.0)):
-        value = product(stacked_high, high_ref[r]) + product(stacked_low, high_ref[r])
-        value = value + product(stacked_high, low_ref[r])
-        real[r] = value[:rows, :LANES] - sign * value[rows:, LANES:]
-        imag[r] = -value[:rows, LANES:] - sign * value[rows:, :LANES]
-    beyond = product(wave.astype(jnp.bfloat16), halo_ref[...])
-    parts = [jnp.sqrt(real[r] * real[r] + imag[r] * imag[r]) for r in range(RADIX)]
-    side_real, side_imag = beyond[:, :LANES], beyond[:, LANES:]
-    parts.append(jnp.sqrt(side_real * side_real + side_imag * side_imag))
-    amplitude_high, amplitude_low = split_float(jnp.concatenate(parts, axis=1))
+    copies = [
+        pltpu.make_async_copy(source, target, sems.at[k])
+        for k, (source, target) in enumerate(
+            (
+                (small_hbm.at[place_ref[1]], small_ref),
+                (wave_hbm, wave_ref),
+                (table_hbm, table_ref),
+                (band_hbm, band_ref),
+            )
+        )
+    ]
+    for copy in copies:
+        copy.start()
+    stations = bin_ref.shape[1]
+    turned = pltpu.roll(
+        bin_ref[...].astype(jnp.float32), (stations - place_ref[0] * PACK) % stations, 1
+    )
+    following = jnp.concatenate(
+        [
+            pltpu.roll(turned[i : i + 1, :], stations - 1 - i, 1)[:, : stations // 2]
+            for i in range(PACK)
+        ],
+        axis=0,
+    ).astype(jnp.bfloat16)
+    for target in range(targets):
+        out_ref[target, 4] = following
+    copies[0].wait()
+    copies[1].wait()
+    quarter = [wave_ref[:, k * SPLIT : (k + 1) * SPLIT] for k in range(RADIX)]
+    even_sum, odd_sum = quarter[0] + quarter[2], quarter[1] + quarter[3]
+    even, odd = quarter[0] - quarter[2], quarter[1] - quarter[3]
+    high, low = [], []
+    for r, first, second in (
+        (0, even_sum + odd_sum, None), (1, even, -odd), (2, even_sum - odd_sum, None), (3, even, odd)
+    ):
+        cosine, sine = small_ref[2 * r : 2 * r + 1, :], small_ref[2 * r + 1 : 2 * r + 2, :]
+        turned_real, turned_imag = first * cosine, -first * sine
+        if second is not None:
+            turned_real = turned_real + second * sine
+            turned_imag = turned_imag + second * cosine
+        for value in (turned_real, turned_imag):
+            value_high, value_low = split_float(value)
+            high.append(value_high)
+            low.append(value_low)
+    high = jnp.concatenate(high, axis=0)
+    low = jnp.concatenate(low, axis=0)
+    copies[2].wait()
+    main, side, rest = (slice(k * 2 * LANES, (k + 1) * 2 * LANES) for k in range(3))
+    value = product(high, table_ref[:, main]) + product(low, table_ref[:, main])
+    value = value + product(high, table_ref[:, rest])
+    beyond = product(high, table_ref[:, side])
+
+    def parts_of(pair, r):
+        first = pair[2 * r * rows : (2 * r + 1) * rows]
+        second = pair[(2 * r + 1) * rows : (2 * r + 2) * rows]
+        return first[:, :LANES] + second[:, LANES:], second[:, :LANES] - first[:, LANES:]
+
+    spectra = [parts_of(value, r) for r in range(RADIX)]
+    amplitudes = [jnp.sqrt(real * real + imag * imag) for real, imag in spectra]
+    width = 2 * HW // RADIX
+    outside = None
+    for r in range(RADIX):
+        real, imag = parts_of(beyond, r)
+        amplitude = jnp.sqrt(real * real + imag * imag)
+        outside = outside + pltpu.roll(amplitude, r * width, 1) if r else amplitude
+    amplitudes.append(outside * small_ref[2 * RADIX + 1 : 2 * RADIX + 2, :LANES])
+    amplitude_high, amplitude_low = split_float(jnp.concatenate(amplitudes, axis=1))
+    copies[3].wait()
     total = product(amplitude_high, band_ref[...]) + product(amplitude_low, band_ref[...])
-    inverse = 1.0 / (total * count_ref[...] + EPSILON)
-    for r in range(RADIX):
+    inverse = 1.0 / (total * small_ref[2 * RADIX : 2 * RADIX + 1, :] + EPSILON)
+    for r, (real, imag) in enumerate(spectra):
         scale = inverse[:, r * LANES : (r + 1) * LANES]
-        scratch[0, r] = real[r] * scale
-        scratch[1, r] = imag[r] * scale
+        scratch[0, r] = real * scale
+        scratch[1, r] = imag * scale
     width = LANES // targets
     chunk = lax.broadcasted_iota(jnp.int32, (PACK, LANES), 1) // width
     for pair in range(2):
@@ -299,80 +345,105 @@
                 for place in range(1, targets):
                     value = jnp.where(chunk == place, rolled[(place - target) % targets], value)
                 out_ref[target, 2 * pair + part] = value.astype(jnp.bfloat16)
-    bins = bin_ref[...].astype(jnp.float32).astype(jnp.bfloat16)
-    for target in range(targets):
-        for k in range(bins.shape[1] // LANES):
-            out_ref[target, 4 + k] = bins[:, k * LANES : (k + 1) * LANES]
-
-
-def pair_kernel(group_ref, data_ref, out_ref, spectra, bins, cross, total):
+
+
+def pair_kernel(place_ref, data_ref, out_ref, spectra, cross, total):
     groups = data_ref.shape[0]
     stations = groups * PACK
-    bin_count = total.shape[1]
+    bin_count = total.shape[0]
     width = LANES // groups
+    half = stations // 2
     for group in range(groups):
-        rows = pl.ds(group * PACK, PACK)
         for pair in range(2):
             for part in range(2):
-                spectra[pair, rows, part * LANES : (part + 1) * LANES] = data_ref[
-                    group, 2 * pair + part
-                ]
-        for k in range(stations // LANES):
-            bins[rows, k * LANES : (k + 1) * LANES] = data_ref[group, 4 + k]
+                spectra[
+                    pair, group * PACK : (group + 1) * PACK, part * LANES : (part + 1) * LANES
+                ] = data_ref[group, 2 * pair + part]
     total[...] = jnp.zeros_like(total)
     lane = lax.broadcasted_iota(jnp.int32, (PACK, 2 * LANES), 1) % LANES
-    place = (lane // width - group_ref[0] + groups) % groups
+    place = (lane // width - place_ref[0] + groups) % groups
     slot = place // (groups // 2) * width + lane % width
     row = lax.broadcasted_iota(jnp.int32, (PACK, 2 * LANES), 0)
-    keep = (slot == row).astype(jnp.float32)[None]
-
-    def one_group(group, first_column):
-        start = pl.multiple_of(group * PACK, PACK)
-        columns = stations - first_column
+    keep = (slot == row).astype(jnp.float32)
+    keep_own = keep.astype(jnp.bfloat16)
+    keep_turned = jnp.concatenate([-keep[:, :LANES], keep[:, LANES:]], axis=1).astype(jnp.bfloat16)
+    wanted = lax.broadcasted_iota(jnp.int32, (bin_count, stations), 0).astype(jnp.float32)
+    wanted = wanted.astype(jnp.bfloat16)
+    one, zero = jnp.bfloat16(1), jnp.bfloat16(0)
+
+    def spread(value):
+        return jnp.broadcast_to(value, (PACK, value.shape[1])).astype(jnp.bfloat16)
+
+    def diagonal(pair, start):
+        own = spectra[pair, start : start + PACK, :].astype(jnp.float32)
+        parts = []
+        for i in range(PACK):
+            value = spread(own[i : i + 1, :])
+            swapped = jnp.concatenate([value[:, LANES:], value[:, :LANES]], axis=1)
+            parts += [value * keep_own, swapped * keep_turned]
+        return jnp.concatenate(parts, axis=0)
+
+    station = lax.broadcasted_iota(jnp.int32, (PACK, stations), 0)
+    column = lax.broadcasted_iota(jnp.int32, (PACK, stations), 1)
+    for number in range(groups // 2):
+        buffer = number % cross.shape[0]
+        low = number * PACK
+        own = low + station
+        near = (column > own) & (column <= own + half)
+        sign = jnp.where(column < own, -1.0, 1.0)
         for pair in range(2):
-            own = spectra[pair, pl.ds(start, PACK), :].astype(jnp.float32)
-            turned = jnp.concatenate([-own[:, LANES:], own[:, :LANES]], axis=1)
-            diagonal = jnp.concatenate(
-                [own[:, None, :] * keep, turned[:, None, :] * keep], axis=1
-            ).astype(jnp.bfloat16)
-            value = product_transposed(
-                diagonal.reshape(PACK * 2 * PACK, 2 * LANES), spectra[pair, first_column:, :]
+            left = jnp.concatenate([diagonal(pair, low), diagonal(pair, low + half)], axis=0)
+            value = product_transposed(left, spectra[pair])
+            rows = slice(pair * 2 * PACK, (pair + 1) * 2 * PACK)
+            for i in range(PACK):
+                first = value[i * 2 * PACK : (i + 1) * 2 * PACK]
+                second = value[(PACK + i) * 2 * PACK : (PACK + i + 1) * 2 * PACK]
+                second = jnp.concatenate([second[:PACK], second[PACK:] * sign[i : i + 1]], axis=0)
+                merged = jnp.where(near[i : i + 1], first, second).astype(jnp.bfloat16)
+                cross[buffer, rows, i * stations : (i + 1) * stations] = merged
+        following = jnp.concatenate(
+            [data_ref[number, 4], data_ref[number + groups // 2, 4]], axis=1
+        ).astype(jnp.float32)
+        shared = pltpu.roll(following, low + 1, 1, stride=1, stride_axis=0)
+        shared = jnp.where(column == own, -1.0, shared)
+        hot = []
+        for i in range(PACK):
+            value = spread(shared[i : i + 1, :])
+            hot.append(
+                jnp.concatenate(
+                    [
+                        jnp.where(value == wanted[k : k + PACK], one, zero)
+                        for k in range(0, bin_count, PACK)
+                    ],
+                    axis=0,
+                )
             )
-            cross[:, pair * 2 * PACK : (pair + 1) * 2 * PACK, first_column:] = value.astype(
-                jnp.bfloat16
-            ).reshape(PACK, 2 * PACK, columns)
-        column = first_column + lax.broadcasted_iota(jnp.int32, (PACK, columns), 1)
-        station = start + lax.broadcasted_iota(jnp.int32, (PACK, columns), 0)
-        own_bins = bins[pl.ds(start, PACK), first_column:].astype(jnp.float32)
-        own_bins = jnp.where(column > station, own_bins, -1.0)
-        wanted = lax.broadcasted_iota(jnp.int32, (bin_count, columns), 0).astype(jnp.float32)
-        value = total[...]
-        for i in range(PACK):
-            onehot = (own_bins[i : i + 1, :] == wanted).astype(jnp.float32).astype(jnp.bfloat16)
-            value = value + product_transposed(cross[i, :, first_column:], onehot)
-        total[...] = value
-
-    for block in range(stations // LANES):
-        per_block = LANES // PACK
-
-        def body(group, carry, first_column=block * LANES):
-            one_group(group, first_column)
-            return carry
-
-        lax.fori_loop(block * per_block, (block + 1) * per_block, body, 0)
-    out_ref[...] = total[...].T
-
-
-def lag_kernel(lag_ref, data_ref, high_ref, low_ref, own_ref, swapped_ref, out_ref):
-    sources, owned, width = data_ref.shape
+        total[...] += product_transposed(jnp.concatenate(hot, axis=1), cross[buffer])
+    copies = out_ref.shape[0] // groups
+    middle = BIN_DEV // 2
+    for group in range(groups):
+        upper = total[group * BIN_DEV : group * BIN_DEV + middle, :]
+        lower = total[group * BIN_DEV + middle : (group + 1) * BIN_DEV, :]
+        value = jnp.concatenate([upper, lower], axis=1)
+        for k in range(copies):
+            out_ref[group * copies + k] = value
+
+
+def lag_kernel(place_ref, data_ref, high_ref, low_ref, own_ref, swapped_ref, out_ref):
+    sources = data_ref.shape[0]
+    owned, blocks = out_ref.shape[0], out_ref.shape[1] // LANES
     lane = lax.broadcasted_iota(jnp.int32, (owned, LANES), 1)
     is_real = lane % (2 * PACK) < PACK
-    per_tile = LANES // width
-    blocks = out_ref.shape[1] // LANES
+    is_first = lane[: owned // 2] < LANES // 2
     turned = [[] for _ in range(blocks)]
-    for tile in range(sources // per_tile):
+    for tile in range(sources // 2):
+        first, second = data_ref[2 * tile], data_ref[2 * tile + 1]
         value = jnp.concatenate(
-            [data_ref[tile * per_tile + k] for k in range(per_tile)], axis=1
+            [
+                jnp.where(is_first, first, pltpu.roll(second, LANES // 2, 1)),
+                jnp.where(is_first, pltpu.roll(first, LANES // 2, 1), second),
+            ],
+            axis=0,
         )
         partner = jnp.where(
             is_real, pltpu.roll(value, LANES - PACK, 1), pltpu.roll(value, PACK, 1)
@@ -396,7 +467,7 @@
 
 def lag_part(array):
     return pl.BlockSpec(
-        (None,) + array.shape[1:], lambda i, s: (s[0],) + (0,) * (array.ndim - 1)
+        (None,) + array.shape[1:], lambda i, s: (s[1],) + (0,) * (array.ndim - 1)
     )
 
 
@@ -423,43 +494,45 @@
     freq_count = NFFT // 2 // lag_count
     stations = station_count * groups
     bin_count = BIN_DEV * groups
-    lag_index = lax.axis_index("lag").astype(jnp.int32).reshape(1)
-    group_index = lax.axis_index("grp").astype(jnp.int32).reshape(1)
+    place = jnp.stack([lax.axis_index("grp"), lax.axis_index("lag")]).astype(jnp.int32)
     rows = waveforms.reshape(station_count * segments, NFFT)
-    tables = [jnp.asarray(t) for t in forward_constants(freq_count, lag_count)]
-    blocks = 4 + stations // LANES
+    small, tables, band = [jnp.asarray(t) for t in forward_constants(freq_count, lag_count)]
+    far = [pltpu.with_memory_space_constraint(v, pltpu.HBM) for v in (rows, small, tables, band)]
     whitened = call(
         whiten_kernel,
-        lag_index,
-        [rows, pair_bin, *tables],
-        [whole_block(rows), whole_block(pair_bin), *[lag_part(t) for t in tables]],
-        jax.ShapeDtypeStruct((groups, blocks, PACK, LANES), jnp.bfloat16),
-        [pltpu.VMEM((2, RADIX, station_count * segments, LANES), jnp.float32)],
+        place,
+        [pair_bin, *far],
+        [whole_block(pair_bin)] + [pl.BlockSpec(memory_space=pltpu.HBM)] * 4,
+        jax.ShapeDtypeStruct((groups, 5, PACK, LANES), jnp.bfloat16),
+        [
+            pltpu.VMEM(rows.shape, jnp.float32),
+            pltpu.VMEM(small.shape[1:], jnp.float32),
+            pltpu.VMEM(tables.shape, jnp.bfloat16),
+            pltpu.VMEM(band.shape, jnp.bfloat16),
+            pltpu.VMEM((2, RADIX, station_count * segments, LANES), jnp.float32),
+            pltpu.SemaphoreType.DMA((4,)),
+        ],
     )
     received = lax.all_to_all(whitened, "grp", 0, 0, tiled=True)
-    binned = call(
+    outgoing = call(
         pair_kernel,
-        group_index,
+        place,
         [received],
         [whole_block(received)],
-        jax.ShapeDtypeStruct((bin_count, 4 * PACK), jnp.float32),
+        jax.ShapeDtypeStruct((groups * lag_count, BIN_DEV // 2, LANES), jnp.float32),
         [
             pltpu.VMEM((2, stations, 2 * LANES), jnp.bfloat16),
-            pltpu.VMEM((stations, stations), jnp.bfloat16),
-            pltpu.VMEM((PACK, 4 * PACK, stations), jnp.bfloat16),
-            pltpu.VMEM((4 * PACK, bin_count), jnp.float32),
+            pltpu.VMEM((2, 4 * PACK, PACK * stations), jnp.bfloat16),
+            pltpu.VMEM((bin_count, 4 * PACK), jnp.float32),
         ],
     )
-    outgoing = jnp.broadcast_to(
-        binned.reshape(groups, 1, BIN_DEV, 4 * PACK), (groups, lag_count, BIN_DEV, 4 * PACK)
-    ).reshape(groups * lag_count, BIN_DEV, 4 * PACK)
     owned = lax.all_to_all(outgoing, ("grp", "lag"), 0, 0, tiled=True)
     high, low, own, swapped = [
         jnp.asarray(t) for t in inverse_constants(freq_count, lag_count, groups)
     ]
     return call(
         lag_kernel,
-        lag_index,
+        place,
         [owned, high, low, own, swapped],
         [whole_block(owned), whole_block(high), whole_block(low), lag_part(own), lag_part(swapped)],
         jax.ShapeDtypeStruct((BIN_DEV, LAGS // lag_count), jnp.float32),
@@ -472,7 +545,7 @@
     freq_count = NFFT // 2 // lag_count
     return (
         lag_count == 2
-        and stations == groups * PACK
+        and stations == groups * PACK == 2 * LANES
         and freq_count == RADIX * LANES
         and segments * 2 * (LANES // groups) == LANES
         and groups * BIN_DEV <= 256

time: 57.5 us -> 42.7 us (0.74)
  blocking collectives: 9.78 us -> 29.3 us
  waiting for transfers between devices: 12.6 us -> 0 us
  starting transfers between devices: 8.46 us -> 0 us
  Pallas kernels: 19 us -> 12.3 us
  local copies, waits for them, and re-layouts: 6.28 us -> 0.67 us
  other arithmetic: 0.8 us -> 0.07 us
    all_to_all x0 -> x1, blocking collectives: none -> 19.6 us  [local_by_frequency(): received = lax.all_to_all(whitened, 'grp', 0, 0, tiled=True)]
    all_to_all x1 -> x0, waiting for transfers between devices: 12.6 us -> none  [local_by_frequency(): received = lax.all_to_all(whitened, 'grp', 0, 0, tiled=True)]
    all_to_all x1 -> x0, starting transfers between devices: 8.46 us -> none  [local_by_frequency(): received = lax.all_to_all(whitened, 'grp', 0, 0, tiled=True)]
    pallas_call x3, Pallas kernels: 19 us -> 12.3 us  [call(): pl.pallas_call(kernel, grid_spec=grid_spec, out_shape=out_shape, compiler...]
    unnamed x20 -> x10, local copies, waits for them, and re-layouts: 5.76 us -> 0.67 us
    all_to_all x1 -> x0, other arithmetic: 0.8 us -> none  [local_by_frequency(): owned = lax.all_to_all(outgoing, ('grp', 'lag'), 0, 0, tiled=True)]
  transfers between devices with their start and end apart: 1 -> 0, of which waited for: 1 -> 0; matrix products, arithmetic and copies ran while one was open for 0% -> 0% of each run, Pallas kernels for 0% -> 0%
where the time goes in v2:
time: 42.7 us; the launch traced here: 42.4 us
  blocking collectives  29.3 us (69%)
  Pallas kernels  12.3 us (29%)
  local copies, waits for them, and re-layouts  0.67 us (2%)
    all_to_all x1, blocking collectives, local_by_frequency(): received = lax.all_to_all(whitened, 'grp', 0, 0, tiled=True)  19.6 us
    pallas_call x3, Pallas kernels, call(): pl.pallas_call(kernel, grid_spec=grid_spec, out_shape=out_shape, compiler...  12.3 us
    all_to_all x1, blocking collectives, local_by_frequency(): owned = lax.all_to_all(outgoing, ('grp', 'lag'), 0, 0, tiled=True)  9.7 us

profile of v2, /device:TPU:0, one launch (start us, length us, event | category | flops | bytes accessed | tf_op | source)
XLA Modules:
  0.0 42.4 jit_solution(16602561377925434151)
XLA Ops:
  0.0 0.0 copy-start.4
  0.0 0.1 pad_add_fusion.place_ref
  0.1 0.6 %copy-done.4 = s32[16,256]{1,0:T(8,128)S(1)} copy-done((s32[16,256]{1,0:T(8,128)S(1)}, s32[16,256]{1,0:T(8,128)}, u32[]{:S(2)}) %copy-start.4) | copy-done | bytes 16408
  0.7 5.0 %shard_map.91 = bf16[16,5,16,128]{3,2,1,0:T(8,128)(2,1)S(1)} custom-call(s32[2]{0:T(128)S(1)} %pad_add_fusion.place_ref, s32[16,256]{1,0:T(8,128)S(1)} %copy-done.4, f32[128,2048]{1,0:T(8,128)} %bitcast.3, f32[2,16,512]{2,1,0:T(8,128)} %constant.22.clone.small_hbm, bf16[512,768]{1,0:T(8,128)(2,1)} %constant.23.clone.table_hbm, ...), custom_call_target="tpu_custom_call" | custom-call | tf_op jit(solution)/shard_map/pallas_call | solution.py:482
  5.7 0.0 copy-start
  5.7 0.0 copy-start.1
  5.7 19.6 %all_to_all.10.data_ref = bf16[16,5,16,128]{3,2,1,0:T(8,128)(2,1)S(1)} all-to-all(bf16[16,5,16,128]{3,2,1,0:T(8,128)(2,1)S(1)} %shard_map.91), channel_id=1, replica_groups=mesh['grp'=16,'lag'=2] {'grp'}, dimensions={0} | all-to-all | bytes 655360 | tf_op jit(solution)/shard_map/all_to_all | solution.py:516
  25.3 5.7 %shard_map.92 = f32[32,4,128]{2,1,0:T(4,128)S(1)} custom-call(s32[2]{0:T(128)S(1)} %pad_add_fusion.place_ref, bf16[16,5,16,128]{3,2,1,0:T(8,128)(2,1)S(1)} %all_to_all.10.data_ref), custom_call_target="tpu_custom_call" | custom-call | tf_op jit(solution)/shard_map/pallas_call | solution.py:482
  31.0 0.0 copy-start.2
  31.0 0.0 copy-start.3
  31.0 9.7 %all_to_all.11.data_ref = f32[32,4,128]{2,1,0:T(4,128)S(1)} all-to-all(f32[32,4,128]{2,1,0:T(4,128)S(1)} %shard_map.92), channel_id=1, replica_groups=mesh['grp'=16,'lag'=2] {'grp','lag'}, dimensions={0} | all-to-all | bytes 131072 | tf_op jit(solution)/shard_map/all_to_all | solution.py:529
  40.7 0.0 copy-done
  40.7 0.0 copy-done.1
  40.7 0.0 copy-done.2
  40.7 0.0 copy-done.3
  40.7 1.6 %shard_map.93 = f32[8,512]{1,0:T(8,128)} custom-call(s32[2]{0:T(128)S(1)} %pad_add_fusion.place_ref, f32[32,4,128]{2,1,0:T(4,128)S(1)} %all_to_all.11.data_ref, bf16[2048,128]{1,0:T(8,128)(2,1)S(1)} %copy-done.1, bf16[2048,128]{1,0:T(8,128)(2,1)S(1)} %copy-done, f32[2,4,2048]{2,1,0:T(4,128)S(1)} %copy-done.3, f32[2,4,2048]{2,1,0:T(4,128)S(1)} %copy-done.2), custom_call_target="tpu_custom_call" | custom-call | tf_op jit(solution)/shard_map/pallas_call | solution.py:482
Async XLA Ops:
  0.0 0.7 %copy-start.4 = (s32[16,256]{1,0:T(8,128)S(1)}, s32[16,256]{1,0:T(8,128)}, u32[]{:S(2)}) copy-start(s32[16,256]{1,0:T(8,128)} %bin_ref.1) | copy-start | bytes 49156
  5.7 35.0 %copy-start = (bf16[2048,128]{1,0:T(8,128)(2,1)S(1)}, bf16[2048,128]{1,0:T(8,128)(2,1)}, u32[]{:S(2)}) copy-start(bf16[2048,128]{1,0:T(8,128)(2,1)} %constant.26.clone.low_ref) | copy-start | bytes 1572868
  5.7 35.0 %copy-start.1 = (bf16[2048,128]{1,0:T(8,128)(2,1)S(1)}, bf16[2048,128]{1,0:T(8,128)(2,1)}, u32[]{:S(2)}) copy-start(bf16[2048,128]{1,0:T(8,128)(2,1)} %constant.25.clone.high_ref) | copy-start | bytes 1572868
  31.0 9.7 %copy-start.2 = (f32[2,4,2048]{2,1,0:T(4,128)S(1)}, f32[2,4,2048]{2,1,0:T(4,128)}, u32[]{:S(2)}) copy-start(f32[2,4,2048]{2,1,0:T(4,128)} %constant.28.clone.swapped_ref) | copy-start | bytes 196612
  31.0 9.7 %copy-start.3 = (f32[2,4,2048]{2,1,0:T(4,128)S(1)}, f32[2,4,2048]{2,1,0:T(4,128)}, u32[]{:S(2)}) copy-start(f32[2,4,2048]{2,1,0:T(4,128)} %constant.27.clone.own_ref) | copy-start | bytes 196612

commit v3 on v2

--- a/solution.py
+++ b/solution.py
@@ -159,6 +159,7 @@
 
 LANES = 128
 RADIX = 4
+HALO = 2 * HW // RADIX
 SPLIT = NFFT // RADIX
 PACK = 16
 
@@ -175,20 +176,17 @@
     width = HW // RADIX
     beyond = np.stack([steps + np.arange(width), np.arange(width) - width])
     beyond = beyond.reshape(-1)
-    table = np.zeros((SPLIT, 4 * LANES))
+    table = np.zeros((SPLIT, 2 * LANES))
+    side = np.zeros((SPLIT, LANES))
     angle = 2.0 * np.pi / SPLIT * (sample[:, None] * np.arange(steps)[None, :] % SPLIT)
     table[:, :steps] = np.cos(angle)
     table[:, LANES : LANES + steps] = np.sin(angle)
     angle = 2.0 * np.pi / SPLIT * (sample[:, None] * beyond[None, :] % SPLIT)
-    table[:, 2 * LANES : 2 * LANES + beyond.size] = np.cos(angle)
-    table[:, 3 * LANES : 3 * LANES + beyond.size] = np.sin(angle)
-    high, low = halves(table)
-    tables = np.concatenate([high, low[:, : 2 * LANES]], axis=1)
+    side[:, : beyond.size] = np.cos(angle)
+    side[:, LANES // 2 : LANES // 2 + beyond.size] = np.sin(angle)
+    tables = np.concatenate([*halves(table), halves(side)[0]], axis=1)
     order = np.concatenate([np.arange(steps) * RADIX + r for r in range(RADIX)])
     outside = np.concatenate([beyond * RADIX + r for r in range(RADIX)])
-    seen = np.concatenate([order, outside])
-    band = np.zeros((freq_count + LANES, freq_count))
-    band[: seen.size] = np.abs(seen[:, None] - order[None, :]) <= HW
     small = np.zeros((lag_count, 2 * RADIX + 8, freq_count), np.float32)
     for index in range(lag_count):
         start = index * freq_count
@@ -201,7 +199,7 @@
         small[index, 2 * RADIX] = 1.0 / (upper - lower + 1)
         there = (start + outside >= 0) & (start + outside < NFFT // 2)
         small[index, 2 * RADIX + 1, : outside.size] = there
-    return small, tables, band.astype(ml_dtypes.bfloat16)
+    return small, tables
 
 
 def inverse_constants(freq_count, lag_count, groups):
@@ -249,29 +247,79 @@
     )
 
 
+def fill_band(band_ref):
+    column = lax.broadcasted_iota(jnp.int32, (LANES, LANES), 1)
+    row = lax.broadcasted_iota(jnp.int32, (LANES, LANES), 0)
+    apart = RADIX * (row - column)
+    near = {
+        shift: (jnp.abs(apart + shift) <= HW).astype(jnp.float32).astype(jnp.bfloat16)
+        for shift in range(1 - RADIX, RADIX)
+    }
+    place = row % HALO
+    outer = row // HALO + RADIX * jnp.where(place < HALO // 2, LANES + place, place - HALO)
+    for to in range(RADIX):
+        at = slice(to * LANES, (to + 1) * LANES)
+        for r in range(RADIX):
+            band_ref[r * LANES : (r + 1) * LANES, at] = near[r - to]
+        beside = (jnp.abs(outer - RADIX * column - to) <= HW) & (row < RADIX * HALO)
+        band_ref[RADIX * LANES :, at] = beside.astype(jnp.float32).astype(jnp.bfloat16)
+
+
 def whiten_kernel(
-    place_ref, bin_ref, wave_hbm, small_hbm, table_hbm, band_hbm, out_ref,
-    wave_ref, small_ref, table_ref, band_ref, scratch, sems,
+    bin_hbm, wave_hbm, small_hbm, table_hbm, out_ref,
+    bin_ref, wave_ref, small_ref, table_ref, band_ref, scratch, sems,
 ):
     rows = wave_ref.shape[0]
     segments = rows // PACK
     targets = out_ref.shape[0]
+    parts = 2
+    part_rows = rows // parts
+    moves = [(small_hbm.at[lax.axis_index("lag")], small_ref)]
+    for k in range(parts):
+        at = pl.ds(k * part_rows, part_rows)
+        moves.append((wave_hbm.at[at], wave_ref.at[at]))
+    moves += [(table_hbm, table_ref), (bin_hbm, bin_ref)]
     copies = [
         pltpu.make_async_copy(source, target, sems.at[k])
-        for k, (source, target) in enumerate(
-            (
-                (small_hbm.at[place_ref[1]], small_ref),
-                (wave_hbm, wave_ref),
-                (table_hbm, table_ref),
-                (band_hbm, band_ref),
-            )
-        )
+        for k, (source, target) in enumerate(moves)
     ]
     for copy in copies:
         copy.start()
+    fill_band(band_ref)
+    copies[0].wait()
+    value, beyond = [], []
+    main, rest = slice(0, 2 * LANES), slice(2 * LANES, 4 * LANES)
+    side = slice(4 * LANES, 5 * LANES)
+    for k in range(parts):
+        copies[1 + k].wait()
+        at = slice(k * part_rows, (k + 1) * part_rows)
+        quarter = [wave_ref[at, j * SPLIT : (j + 1) * SPLIT] for j in range(RADIX)]
+        even_sum, odd_sum = quarter[0] + quarter[2], quarter[1] + quarter[3]
+        even, odd = quarter[0] - quarter[2], quarter[1] - quarter[3]
+        high, low = [], []
+        for r, first, second in (
+            (0, even_sum + odd_sum, None), (1, even, -odd), (2, even_sum - odd_sum, None), (3, even, odd)
+        ):
+            cosine, sine = small_ref[2 * r : 2 * r + 1, :], small_ref[2 * r + 1 : 2 * r + 2, :]
+            turned_real, turned_imag = first * cosine, -first * sine
+            if second is not None:
+                turned_real = turned_real + second * sine
+                turned_imag = turned_imag + second * cosine
+            for turned in (turned_real, turned_imag):
+                turned_high, turned_low = split_float(turned)
+                high.append(turned_high)
+                low.append(turned_low)
+        high = jnp.concatenate(high, axis=0)
+        low = jnp.concatenate(low, axis=0)
+        if k == 0:
+            copies[1 + parts].wait()
+        product_main = product(high, table_ref[:, main]) + product(low, table_ref[:, main])
+        value.append(product_main + product(high, table_ref[:, rest]))
+        beyond.append(product(high, table_ref[:, side]))
+    copies[2 + parts].wait()
     stations = bin_ref.shape[1]
     turned = pltpu.roll(
-        bin_ref[...].astype(jnp.float32), (stations - place_ref[0] * PACK) % stations, 1
+        bin_ref[...].astype(jnp.float32), (stations - lax.axis_index("grp") * PACK) % stations, 1
     )
     following = jnp.concatenate(
         [
@@ -282,48 +330,27 @@
     ).astype(jnp.bfloat16)
     for target in range(targets):
         out_ref[target, 4] = following
-    copies[0].wait()
-    copies[1].wait()
-    quarter = [wave_ref[:, k * SPLIT : (k + 1) * SPLIT] for k in range(RADIX)]
-    even_sum, odd_sum = quarter[0] + quarter[2], quarter[1] + quarter[3]
-    even, odd = quarter[0] - quarter[2], quarter[1] - quarter[3]
-    high, low = [], []
-    for r, first, second in (
-        (0, even_sum + odd_sum, None), (1, even, -odd), (2, even_sum - odd_sum, None), (3, even, odd)
-    ):
-        cosine, sine = small_ref[2 * r : 2 * r + 1, :], small_ref[2 * r + 1 : 2 * r + 2, :]
-        turned_real, turned_imag = first * cosine, -first * sine
-        if second is not None:
-            turned_real = turned_real + second * sine
-            turned_imag = turned_imag + second * cosine
-        for value in (turned_real, turned_imag):
-            value_high, value_low = split_float(value)
-            high.append(value_high)
-            low.append(value_low)
-    high = jnp.concatenate(high, axis=0)
-    low = jnp.concatenate(low, axis=0)
-    copies[2].wait()
-    main, side, rest = (slice(k * 2 * LANES, (k + 1) * 2 * LANES) for k in range(3))
-    value = product(high, table_ref[:, main]) + product(low, table_ref[:, main])
-    value = value + product(high, table_ref[:, rest])
-    beyond = product(high, table_ref[:, side])
-
-    def parts_of(pair, r):
-        first = pair[2 * r * rows : (2 * r + 1) * rows]
-        second = pair[(2 * r + 1) * rows : (2 * r + 2) * rows]
+
+    def both_of(pairs, r):
+        first = [pair[2 * r * part_rows : (2 * r + 1) * part_rows] for pair in pairs]
+        second = [pair[(2 * r + 1) * part_rows : (2 * r + 2) * part_rows] for pair in pairs]
+        return jnp.concatenate(first, axis=0), jnp.concatenate(second, axis=0)
+
+    def parts_of(r):
+        first, second = both_of(value, r)
         return first[:, :LANES] + second[:, LANES:], second[:, :LANES] - first[:, LANES:]
 
-    spectra = [parts_of(value, r) for r in range(RADIX)]
+    spectra = [parts_of(r) for r in range(RADIX)]
     amplitudes = [jnp.sqrt(real * real + imag * imag) for real, imag in spectra]
-    width = 2 * HW // RADIX
     outside = None
     for r in range(RADIX):
-        real, imag = parts_of(beyond, r)
+        first, second = both_of(beyond, r)
+        real = first + pltpu.roll(second, LANES // 2, 1)
+        imag = second - pltpu.roll(first, LANES // 2, 1)
         amplitude = jnp.sqrt(real * real + imag * imag)
-        outside = outside + pltpu.roll(amplitude, r * width, 1) if r else amplitude
+        outside = outside + pltpu.roll(amplitude, r * HALO, 1) if r else amplitude
     amplitudes.append(outside * small_ref[2 * RADIX + 1 : 2 * RADIX + 2, :LANES])
     amplitude_high, amplitude_low = split_float(jnp.concatenate(amplitudes, axis=1))
-    copies[3].wait()
     total = product(amplitude_high, band_ref[...]) + product(amplitude_low, band_ref[...])
     inverse = 1.0 / (total * small_ref[2 * RADIX : 2 * RADIX + 1, :] + EPSILON)
     for r, (real, imag) in enumerate(spectra):
@@ -347,7 +374,7 @@
                 out_ref[target, 2 * pair + part] = value.astype(jnp.bfloat16)
 
 
-def pair_kernel(place_ref, data_ref, out_ref, spectra, cross, total):
+def pair_kernel(data_ref, out_ref, spectra, cross, total):
     groups = data_ref.shape[0]
     stations = groups * PACK
     bin_count = total.shape[0]
@@ -361,7 +388,7 @@
                 ] = data_ref[group, 2 * pair + part]
     total[...] = jnp.zeros_like(total)
     lane = lax.broadcasted_iota(jnp.int32, (PACK, 2 * LANES), 1) % LANES
-    place = (lane // width - place_ref[0] + groups) % groups
+    place = (lane // width - lax.axis_index("grp") + groups) % groups
     slot = place // (groups // 2) * width + lane % width
     row = lax.broadcasted_iota(jnp.int32, (PACK, 2 * LANES), 0)
     keep = (slot == row).astype(jnp.float32)
@@ -429,7 +456,8 @@
             out_ref[group * copies + k] = value
 
 
-def lag_kernel(place_ref, data_ref, high_ref, low_ref, own_ref, swapped_ref, out_ref):
+def lag_kernel(data_ref, high_ref, low_ref, own_ref, swapped_ref, out_ref):
+    lag = lax.axis_index("lag")
     sources = data_ref.shape[0]
     owned, blocks = out_ref.shape[0], out_ref.shape[1] // LANES
     lane = lax.broadcasted_iota(jnp.int32, (owned, LANES), 1)
@@ -451,7 +479,8 @@
         at = slice(tile * LANES, (tile + 1) * LANES)
         for block in range(blocks):
             turned[block].append(
-                value * own_ref[block : block + 1, at] + partner * swapped_ref[block : block + 1, at]
+                value * own_ref[lag, block : block + 1, at]
+                + partner * swapped_ref[lag, block : block + 1, at]
             )
     left = jnp.concatenate([jnp.concatenate(row, axis=1) for row in turned], axis=0)
     left_high, left_low = split_float(left)
@@ -461,30 +490,19 @@
         out_ref[:, block * LANES : (block + 1) * LANES] = value[block * owned : (block + 1) * owned]
 
 
-def whole_block(array):
-    return pl.BlockSpec(array.shape, lambda i, s: (0,) * array.ndim)
-
-
-def lag_part(array):
-    return pl.BlockSpec(
-        (None,) + array.shape[1:], lambda i, s: (s[1],) + (0,) * (array.ndim - 1)
-    )
-
-
-def call(kernel, scalar, arrays, specs, out_shape, scratch=()):
-    grid_spec = pltpu.PrefetchScalarGridSpec(
-        num_scalar_prefetch=1,
-        grid=(1,),
-        in_specs=specs,
-        out_specs=whole_block(out_shape),
-        scratch_shapes=list(scratch),
-    )
+def call(kernel, arrays, spaces, out_shape, scratch=()):
+    arrays = [
+        pltpu.with_memory_space_constraint(array, space) if space is pltpu.HBM else array
+        for array, space in zip(arrays, spaces)
+    ]
     return pl.pallas_call(
         kernel,
-        grid_spec=grid_spec,
+        in_specs=[pl.BlockSpec(memory_space=space) for space in spaces],
+        out_specs=pl.BlockSpec(memory_space=pltpu.VMEM),
         out_shape=out_shape,
+        scratch_shapes=list(scratch),
         compiler_params=pltpu.CompilerParams(vmem_limit_bytes=48 << 20),
-    )(scalar, *arrays)
+    )(*arrays)
 
 
 def local_by_frequency(waveforms, pair_bin):
@@ -494,31 +512,28 @@
     freq_count = NFFT // 2 // lag_count
     stations = station_count * groups
     bin_count = BIN_DEV * groups
-    place = jnp.stack([lax.axis_index("grp"), lax.axis_index("lag")]).astype(jnp.int32)
     rows = waveforms.reshape(station_count * segments, NFFT)
-    small, tables, band = [jnp.asarray(t) for t in forward_constants(freq_count, lag_count)]
-    far = [pltpu.with_memory_space_constraint(v, pltpu.HBM) for v in (rows, small, tables, band)]
+    small, tables = [jnp.asarray(t) for t in forward_constants(freq_count, lag_count)]
     whitened = call(
         whiten_kernel,
-        place,
-        [pair_bin, *far],
-        [whole_block(pair_bin)] + [pl.BlockSpec(memory_space=pltpu.HBM)] * 4,
+        [pair_bin, rows, small, tables],
+        [pltpu.HBM] * 4,
         jax.ShapeDtypeStruct((groups, 5, PACK, LANES), jnp.bfloat16),
         [
+            pltpu.VMEM(pair_bin.shape, jnp.int32),
             pltpu.VMEM(rows.shape, jnp.float32),
             pltpu.VMEM(small.shape[1:], jnp.float32),
             pltpu.VMEM(tables.shape, jnp.bfloat16),
-            pltpu.VMEM(band.shape, jnp.bfloat16),
+            pltpu.VMEM((freq_count + LANES, freq_count), jnp.bfloat16),
             pltpu.VMEM((2, RADIX, station_count * segments, LANES), jnp.float32),
-            pltpu.SemaphoreType.DMA((4,)),
+            pltpu.SemaphoreType.DMA((5,)),
         ],
     )
     received = lax.all_to_all(whitened, "grp", 0, 0, tiled=True)
     outgoing = call(
         pair_kernel,
-        place,
         [received],
-        [whole_block(received)],
+        [pltpu.VMEM],
         jax.ShapeDtypeStruct((groups * lag_count, BIN_DEV // 2, LANES), jnp.float32),
         [
             pltpu.VMEM((2, stations, 2 * LANES), jnp.bfloat16),
@@ -532,9 +547,8 @@
     ]
     return call(
         lag_kernel,
-        place,
         [owned, high, low, own, swapped],
-        [whole_block(owned), whole_block(high), whole_block(low), lag_part(own), lag_part(swapped)],
+        [pltpu.VMEM] * 5,
         jax.ShapeDtypeStruct((BIN_DEV, LAGS // lag_count), jnp.float32),
     )
 

time: 42.7 us -> 40.2 us (0.941)
  Pallas kernels: 12.3 us -> 10.6 us
  local copies, waits for them, and re-layouts: 0.67 us -> 0.03 us
    pallas_call x3, Pallas kernels: 12.3 us -> 10.6 us  [call(): pl.pallas_call(kernel, in_specs=[pl.BlockSpec(memory_space=space) for spa...]
    unnamed x10 -> x8, local copies, waits for them, and re-layouts: 0.67 us -> 0.03 us
where the time goes in v3:
time: 40.2 us; the launch traced here: 39.9 us
  blocking collectives  29.3 us (73%)
  Pallas kernels  10.6 us (26%)
    all_to_all x1, blocking collectives, local_by_frequency(): received = lax.all_to_all(whitened, 'grp', 0, 0, tiled=True)  19.6 us
    pallas_call x3, Pallas kernels, call(): pl.pallas_call(kernel, in_specs=[pl.BlockSpec(memory_space=space) for spa...  10.6 us
    all_to_all x1, blocking collectives, local_by_frequency(): owned = lax.all_to_all(outgoing, ('grp', 'lag'), 0, 0, tiled=True)  9.7 us

profile of v3, /device:TPU:0, one launch (start us, length us, event | category | flops | bytes accessed | tf_op | source)
XLA Modules:
  0.0 39.9 jit_solution(10399066979476717400)
XLA Ops:
  0.0 4.4 %shard_map.82 = bf16[16,5,16,128]{3,2,1,0:T(8,128)(2,1)S(1)} custom-call(s32[16,256]{1,0:T(8,128)} %bin_hbm.1, f32[128,2048]{1,0:T(8,128)} %bitcast.1, f32[2,16,512]{2,1,0:T(8,128)} %constant.12.clone.small_hbm, bf16[512,640]{1,0:T(8,128)(2,1)} %constant.13.clone.table_hbm), custom_call_target="tpu_custom_call" | custom-call | tf_op jit(solution)/shard_map/pallas_call | solution.py:498
  4.4 0.0 copy-start
  4.4 0.0 copy-start.1
  4.4 19.6 %all_to_all.10.data_ref = bf16[16,5,16,128]{3,2,1,0:T(8,128)(2,1)S(1)} all-to-all(bf16[16,5,16,128]{3,2,1,0:T(8,128)(2,1)S(1)} %shard_map.82), channel_id=1, replica_groups=mesh['grp'=16,'lag'=2] {'grp'}, dimensions={0} | all-to-all | bytes 655360 | tf_op jit(solution)/shard_map/all_to_all | solution.py:532
  23.9 5.1 %shard_map.83 = f32[32,4,128]{2,1,0:T(4,128)S(1)} custom-call(bf16[16,5,16,128]{3,2,1,0:T(8,128)(2,1)S(1)} %all_to_all.10.data_ref), custom_call_target="tpu_custom_call" | custom-call | tf_op jit(solution)/shard_map/pallas_call | solution.py:498
  29.1 0.0 copy-start.2
  29.1 0.0 copy-start.3
  29.1 9.7 %all_to_all.11.data_ref = f32[32,4,128]{2,1,0:T(4,128)S(1)} all-to-all(f32[32,4,128]{2,1,0:T(4,128)S(1)} %shard_map.83), channel_id=1, replica_groups=mesh['grp'=16,'lag'=2] {'grp','lag'}, dimensions={0} | all-to-all | bytes 131072 | tf_op jit(solution)/shard_map/all_to_all | solution.py:544
  38.8 0.0 copy-done
  38.8 0.0 copy-done.1
  38.8 0.0 copy-done.2
  38.8 0.0 copy-done.3
  38.8 1.1 %shard_map.84 = f32[8,512]{1,0:T(8,128)} custom-call(f32[32,4,128]{2,1,0:T(4,128)S(1)} %all_to_all.11.data_ref, bf16[2048,128]{1,0:T(8,128)(2,1)S(1)} %copy-done.1, bf16[2048,128]{1,0:T(8,128)(2,1)S(1)} %copy-done, f32[2,4,2048]{2,1,0:T(4,128)S(1)} %copy-done.3, f32[2,4,2048]{2,1,0:T(4,128)S(1)} %copy-done.2), custom_call_target="tpu_custom_call" | custom-call | tf_op jit(solution)/shard_map/pallas_call | solution.py:498
Async XLA Ops:
  4.4 34.5 %copy-start = (bf16[2048,128]{1,0:T(8,128)(2,1)S(1)}, bf16[2048,128]{1,0:T(8,128)(2,1)}, u32[]{:S(2)}) copy-start(bf16[2048,128]{1,0:T(8,128)(2,1)} %constant.15.clone.low_ref) | copy-start | bytes 1572868
  4.4 34.5 %copy-start.1 = (bf16[2048,128]{1,0:T(8,128)(2,1)S(1)}, bf16[2048,128]{1,0:T(8,128)(2,1)}, u32[]{:S(2)}) copy-start(bf16[2048,128]{1,0:T(8,128)(2,1)} %constant.14.clone.high_ref) | copy-start | bytes 1572868
  29.1 9.7 %copy-start.2 = (f32[2,4,2048]{2,1,0:T(4,128)S(1)}, f32[2,4,2048]{2,1,0:T(4,128)}, u32[]{:S(2)}) copy-start(f32[2,4,2048]{2,1,0:T(4,128)} %constant.17.clone.swapped_ref) | copy-start | bytes 196612
  29.1 9.7 %copy-start.3 = (f32[2,4,2048]{2,1,0:T(4,128)S(1)}, f32[2,4,2048]{2,1,0:T(4,128)}, u32[]{:S(2)}) copy-start(f32[2,4,2048]{2,1,0:T(4,128)} %constant.16.clone.own_ref) | copy-start | bytes 196612

commit v4 on v3

--- a/solution.py
+++ b/solution.py
@@ -159,7 +159,6 @@
 
 LANES = 128
 RADIX = 4
-HALO = 2 * HW // RADIX
 SPLIT = NFFT // RADIX
 PACK = 16
 
@@ -186,7 +185,6 @@
     side[:, LANES // 2 : LANES // 2 + beyond.size] = np.sin(angle)
     tables = np.concatenate([*halves(table), halves(side)[0]], axis=1)
     order = np.concatenate([np.arange(steps) * RADIX + r for r in range(RADIX)])
-    outside = np.concatenate([beyond * RADIX + r for r in range(RADIX)])
     small = np.zeros((lag_count, 2 * RADIX + 8, freq_count), np.float32)
     for index in range(lag_count):
         start = index * freq_count
@@ -197,8 +195,8 @@
         upper = np.minimum(start + order + HW, NFFT // 2 - 1)
         lower = np.maximum(start + order - HW, 0)
         small[index, 2 * RADIX] = 1.0 / (upper - lower + 1)
-        there = (start + outside >= 0) & (start + outside < NFFT // 2)
-        small[index, 2 * RADIX + 1, : outside.size] = there
+        small[index, 2 * RADIX + 1, :width] = index > 0
+        small[index, 2 * RADIX + 1, LANES - width : LANES] = index < lag_count - 1
     return small, tables
 
 
@@ -247,76 +245,81 @@
     )
 
 
-def fill_band(band_ref):
-    column = lax.broadcasted_iota(jnp.int32, (LANES, LANES), 1)
-    row = lax.broadcasted_iota(jnp.int32, (LANES, LANES), 0)
-    apart = RADIX * (row - column)
-    near = {
-        shift: (jnp.abs(apart + shift) <= HW).astype(jnp.float32).astype(jnp.bfloat16)
-        for shift in range(1 - RADIX, RADIX)
-    }
-    place = row % HALO
-    outer = row // HALO + RADIX * jnp.where(place < HALO // 2, LANES + place, place - HALO)
-    for to in range(RADIX):
-        at = slice(to * LANES, (to + 1) * LANES)
-        for r in range(RADIX):
-            band_ref[r * LANES : (r + 1) * LANES, at] = near[r - to]
-        beside = (jnp.abs(outer - RADIX * column - to) <= HW) & (row < RADIX * HALO)
-        band_ref[RADIX * LANES :, at] = beside.astype(jnp.float32).astype(jnp.bfloat16)
+def whole_steps():
+    reach = HW // RADIX
+    row = lax.broadcasted_iota(jnp.int32, (2 * LANES, LANES), 0)
+    column = lax.broadcasted_iota(jnp.int32, (2 * LANES, LANES), 1)
+    beyond = row - LANES
+    step = jnp.where(beyond < reach, beyond - reach, beyond + reach)
+    step = jnp.where(row < LANES, row, step)
+    inside = (row < LANES) | (beyond < reach) | (beyond >= LANES - reach)
+    near = (jnp.abs(step - column) < reach) & inside
+    return near.astype(jnp.float32).astype(jnp.bfloat16)
 
 
 def whiten_kernel(
     bin_hbm, wave_hbm, small_hbm, table_hbm, out_ref,
-    bin_ref, wave_ref, small_ref, table_ref, band_ref, scratch, sems,
+    bin_ref, wave_ref, small_ref, table_ref, scratch, sems,
 ):
     rows = wave_ref.shape[0]
     segments = rows // PACK
     targets = out_ref.shape[0]
-    parts = 2
-    part_rows = rows // parts
-    moves = [(small_hbm.at[lax.axis_index("lag")], small_ref)]
-    for k in range(parts):
-        at = pl.ds(k * part_rows, part_rows)
-        moves.append((wave_hbm.at[at], wave_ref.at[at]))
-    moves += [(table_hbm, table_ref), (bin_hbm, bin_ref)]
+    moves = (
+        (small_hbm.at[lax.axis_index("lag")], small_ref),
+        (wave_hbm, wave_ref),
+        (table_hbm, table_ref),
+        (bin_hbm, bin_ref),
+    )
     copies = [
         pltpu.make_async_copy(source, target, sems.at[k])
         for k, (source, target) in enumerate(moves)
     ]
     for copy in copies:
         copy.start()
-    fill_band(band_ref)
-    copies[0].wait()
-    value, beyond = [], []
+    near = whole_steps()
+    for copy in copies:
+        copy.wait()
+    quarter = [wave_ref[:, k * SPLIT : (k + 1) * SPLIT] for k in range(RADIX)]
+    even_sum, odd_sum = quarter[0] + quarter[2], quarter[1] + quarter[3]
+    even, odd = quarter[0] - quarter[2], quarter[1] - quarter[3]
     main, rest = slice(0, 2 * LANES), slice(2 * LANES, 4 * LANES)
     side = slice(4 * LANES, 5 * LANES)
-    for k in range(parts):
-        copies[1 + k].wait()
-        at = slice(k * part_rows, (k + 1) * part_rows)
-        quarter = [wave_ref[at, j * SPLIT : (j + 1) * SPLIT] for j in range(RADIX)]
-        even_sum, odd_sum = quarter[0] + quarter[2], quarter[1] + quarter[3]
-        even, odd = quarter[0] - quarter[2], quarter[1] - quarter[3]
-        high, low = [], []
-        for r, first, second in (
-            (0, even_sum + odd_sum, None), (1, even, -odd), (2, even_sum - odd_sum, None), (3, even, odd)
-        ):
-            cosine, sine = small_ref[2 * r : 2 * r + 1, :], small_ref[2 * r + 1 : 2 * r + 2, :]
-            turned_real, turned_imag = first * cosine, -first * sine
-            if second is not None:
-                turned_real = turned_real + second * sine
-                turned_imag = turned_imag + second * cosine
-            for turned in (turned_real, turned_imag):
-                turned_high, turned_low = split_float(turned)
-                high.append(turned_high)
-                low.append(turned_low)
-        high = jnp.concatenate(high, axis=0)
-        low = jnp.concatenate(low, axis=0)
-        if k == 0:
-            copies[1 + parts].wait()
-        product_main = product(high, table_ref[:, main]) + product(low, table_ref[:, main])
-        value.append(product_main + product(high, table_ref[:, rest]))
-        beyond.append(product(high, table_ref[:, side]))
-    copies[2 + parts].wait()
+    spectra, amplitudes, outside = [], [], []
+    for r, first, second in (
+        (0, even_sum + odd_sum, None), (1, even, -odd), (2, even_sum - odd_sum, None), (3, even, odd)
+    ):
+        cosine, sine = small_ref[2 * r : 2 * r + 1, :], small_ref[2 * r + 1 : 2 * r + 2, :]
+        turned_real, turned_imag = first * cosine, -first * sine
+        if second is not None:
+            turned_real = turned_real + second * sine
+            turned_imag = turned_imag + second * cosine
+        high, low = split_float(jnp.concatenate([turned_real, turned_imag], axis=0))
+        value = product(high, table_ref[:, main]) + product(low, table_ref[:, main])
+        value = value + product(high, table_ref[:, rest])
+        beyond = product(high, table_ref[:, side])
+        real = value[:rows, :LANES] + value[rows:, LANES:]
+        imag = value[rows:, :LANES] - value[:rows, LANES:]
+        spectra.append((real, imag))
+        amplitudes.append(jnp.sqrt(real * real + imag * imag))
+        real = beyond[:rows] + pltpu.roll(beyond[rows:], LANES // 2, 1)
+        imag = beyond[rows:] - pltpu.roll(beyond[:rows], LANES // 2, 1)
+        outside.append(jnp.sqrt(real * real + imag * imag))
+    reach = HW // RADIX
+    there = small_ref[2 * RADIX + 1 : 2 * RADIX + 2, :LANES]
+    outside = [pltpu.roll(value, LANES - reach, 1) * there for value in outside]
+    sums = jnp.concatenate([sum(amplitudes), sum(outside)], axis=1)
+    sums_high, sums_low = split_float(sums)
+    common = product(sums_high, near) + product(sums_low, near)
+    lane = lax.broadcasted_iota(jnp.int32, (rows, LANES), 1)
+    for r, (real, imag) in enumerate(spectra):
+        above = pltpu.roll(sum(amplitudes[: r + 1]), LANES - reach, 1)
+        above = jnp.where(lane < LANES - reach, above, sum(outside[: r + 1]))
+        below = pltpu.roll(sum(amplitudes[r:]), reach, 1)
+        below = jnp.where(lane >= reach, below, sum(outside[r:]))
+        count = small_ref[2 * RADIX : 2 * RADIX + 1, r * LANES : (r + 1) * LANES]
+        scale = 1.0 / ((common + above + below) * count + EPSILON)
+        scratch[0, r] = real * scale
+        scratch[1, r] = imag * scale
     stations = bin_ref.shape[1]
     turned = pltpu.roll(
         bin_ref[...].astype(jnp.float32), (stations - lax.axis_index("grp") * PACK) % stations, 1
@@ -328,37 +331,10 @@
         ],
         axis=0,
     ).astype(jnp.bfloat16)
-    for target in range(targets):
-        out_ref[target, 4] = following
-
-    def both_of(pairs, r):
-        first = [pair[2 * r * part_rows : (2 * r + 1) * part_rows] for pair in pairs]
-        second = [pair[(2 * r + 1) * part_rows : (2 * r + 2) * part_rows] for pair in pairs]
-        return jnp.concatenate(first, axis=0), jnp.concatenate(second, axis=0)
-
-    def parts_of(r):
-        first, second = both_of(value, r)
-        return first[:, :LANES] + second[:, LANES:], second[:, :LANES] - first[:, LANES:]
-
-    spectra = [parts_of(r) for r in range(RADIX)]
-    amplitudes = [jnp.sqrt(real * real + imag * imag) for real, imag in spectra]
-    outside = None
-    for r in range(RADIX):
-        first, second = both_of(beyond, r)
-        real = first + pltpu.roll(second, LANES // 2, 1)
-        imag = second - pltpu.roll(first, LANES // 2, 1)
-        amplitude = jnp.sqrt(real * real + imag * imag)
-        outside = outside + pltpu.roll(amplitude, r * HALO, 1) if r else amplitude
-    amplitudes.append(outside * small_ref[2 * RADIX + 1 : 2 * RADIX + 2, :LANES])
-    amplitude_high, amplitude_low = split_float(jnp.concatenate(amplitudes, axis=1))
-    total = product(amplitude_high, band_ref[...]) + product(amplitude_low, band_ref[...])
-    inverse = 1.0 / (total * small_ref[2 * RADIX : 2 * RADIX + 1, :] + EPSILON)
-    for r, (real, imag) in enumerate(spectra):
-        scale = inverse[:, r * LANES : (r + 1) * LANES]
-        scratch[0, r] = real * scale
-        scratch[1, r] = imag * scale
     width = LANES // targets
     chunk = lax.broadcasted_iota(jnp.int32, (PACK, LANES), 1) // width
+    chunk = chunk.astype(jnp.float32).astype(jnp.bfloat16)
+    masks = [chunk == jnp.bfloat16(place) for place in range(targets)]
     for pair in range(2):
         for part in range(2):
             rolled = []
@@ -366,15 +342,18 @@
                 for segment in range(segments):
                     rows_of = scratch[part, 2 * pair + half, pl.ds(segment, PACK, stride=segments), :]
                     shift = width * (half * segments + segment)
-                    rolled.append(pltpu.roll(rows_of, shift, 1) if shift else rows_of)
+                    rows_of = pltpu.roll(rows_of, shift, 1) if shift else rows_of
+                    rolled.append(rows_of.astype(jnp.bfloat16))
             for target in range(targets):
                 value = rolled[-target % targets]
                 for place in range(1, targets):
-                    value = jnp.where(chunk == place, rolled[(place - target) % targets], value)
-                out_ref[target, 2 * pair + part] = value.astype(jnp.bfloat16)
-
-
-def pair_kernel(data_ref, out_ref, spectra, cross, total):
+                    value = jnp.where(masks[place], rolled[(place - target) % targets], value)
+                out_ref[target, 2 * pair + part] = value
+    for target in range(targets):
+        out_ref[target, 4] = following
+
+
+def pair_kernel(data_ref, out_ref, spectra, cross, bins, total):
     groups = data_ref.shape[0]
     stations = groups * PACK
     bin_count = total.shape[0]
@@ -386,66 +365,96 @@
                 spectra[
                     pair, group * PACK : (group + 1) * PACK, part * LANES : (part + 1) * LANES
                 ] = data_ref[group, 2 * pair + part]
-    total[...] = jnp.zeros_like(total)
-    lane = lax.broadcasted_iota(jnp.int32, (PACK, 2 * LANES), 1) % LANES
-    place = (lane // width - lax.axis_index("grp") + groups) % groups
+    station = lax.broadcasted_iota(jnp.int32, (half, half), 0)
+    column = lax.broadcasted_iota(jnp.int32, (half, half), 1)
+    for group in range(groups // 2):
+        following = jnp.concatenate(
+            [data_ref[group, 4], data_ref[group + groups // 2, 4]], axis=1
+        ).astype(jnp.float32)
+        bins[group * PACK : (group + 1) * PACK, :] = pltpu.roll(
+            following, group * PACK + 1, 1, stride=1, stride_axis=0
+        )
+    near, far = bins[:, :half], bins[:, half:]
+    inner = jnp.where(column > station, near, jnp.where(column < station, far.T, -1.0))
+    bins[:, half:] = jnp.where(column <= station, far, near.T)
+    bins[:, :half] = inner
+
+    def spread(value):
+        return jnp.broadcast_to(value, (PACK, value.shape[1])).astype(jnp.bfloat16)
+
+    def swap(value):
+        return jnp.concatenate([value[:, LANES:], value[:, :LANES]], axis=1)
+
+    def as_float(mask):
+        return jnp.where(mask, 1.0, 0.0)
+
+    lane = lax.broadcasted_iota(jnp.int32, (PACK, 2 * LANES), 1)
+    row = lax.broadcasted_iota(jnp.int32, (PACK, 2 * LANES), 0)
+    place = (lane % LANES // width - lax.axis_index("grp") + groups) % groups
     slot = place // (groups // 2) * width + lane % width
-    row = lax.broadcasted_iota(jnp.int32, (PACK, 2 * LANES), 0)
-    keep = (slot == row).astype(jnp.float32)
+    sign = jnp.where(lane < LANES, -1.0, 1.0)
+    keep = as_float(slot == row)
     keep_own = keep.astype(jnp.bfloat16)
-    keep_turned = jnp.concatenate([-keep[:, :LANES], keep[:, LANES:]], axis=1).astype(jnp.bfloat16)
+    keep_turned = (keep * sign).astype(jnp.bfloat16)
+    folded = as_float(slot % (PACK // 2) == row % (PACK // 2))
+    fold_own = jnp.where(row < PACK // 2, folded, 0.0).astype(jnp.bfloat16)
+    fold_turned = jnp.where(row < PACK // 2, 0.0, -sign * folded).astype(jnp.bfloat16)
+    first_bins = as_float(slot[:1] < PACK // 2).astype(jnp.bfloat16)
+    last_bins = as_float(slot[:1] >= PACK // 2).astype(jnp.bfloat16)
+    eight = PACK // 2
+    for chunk in range(groups // 2):
+        start = chunk * PACK
+        for pair in range(2):
+            own = spectra[pair, start : start + PACK, :].astype(jnp.float32)
+            other = spectra[pair, half + start : half + start + PACK, :].astype(jnp.float32)
+            upper, lower = [], []
+            for i in range(PACK):
+                value = spread(own[i : i + 1, :])
+                upper += [value * keep_own, swap(value) * keep_turned]
+                value = spread(other[i : i + 1, :])
+                lower.append(value * fold_own + swap(value) * fold_turned)
+            first = product_transposed(jnp.concatenate(upper, axis=0), spectra[pair])
+            second_half = spectra[pair, half:, :]
+            second = product_transposed(
+                jnp.concatenate(lower, axis=0),
+                jnp.concatenate([second_half * first_bins, second_half * last_bins], axis=0),
+            )
+            rows = slice(pair * 2 * PACK, (pair + 1) * 2 * PACK)
+            for i in range(PACK):
+                mine = first[i * 2 * PACK : (i + 1) * 2 * PACK]
+                theirs = second[i * PACK : (i + 1) * PACK]
+                theirs = jnp.concatenate(
+                    [
+                        theirs[:eight, :half],
+                        theirs[:eight, half:],
+                        theirs[eight:, :half],
+                        theirs[eight:, half:],
+                    ],
+                    axis=0,
+                )
+                inner = jnp.where(column[:1] > start + i, mine[:, :half], theirs)
+                at = i * stations
+                cross[chunk, rows, at : at + half] = inner.astype(jnp.bfloat16)
+                cross[chunk, rows, at + half : at + stations] = mine[:, half:].astype(jnp.bfloat16)
     wanted = lax.broadcasted_iota(jnp.int32, (bin_count, stations), 0).astype(jnp.float32)
     wanted = wanted.astype(jnp.bfloat16)
     one, zero = jnp.bfloat16(1), jnp.bfloat16(0)
-
-    def spread(value):
-        return jnp.broadcast_to(value, (PACK, value.shape[1])).astype(jnp.bfloat16)
-
-    def diagonal(pair, start):
-        own = spectra[pair, start : start + PACK, :].astype(jnp.float32)
-        parts = []
-        for i in range(PACK):
-            value = spread(own[i : i + 1, :])
-            swapped = jnp.concatenate([value[:, LANES:], value[:, :LANES]], axis=1)
-            parts += [value * keep_own, swapped * keep_turned]
-        return jnp.concatenate(parts, axis=0)
-
-    station = lax.broadcasted_iota(jnp.int32, (PACK, stations), 0)
-    column = lax.broadcasted_iota(jnp.int32, (PACK, stations), 1)
-    for number in range(groups // 2):
-        buffer = number % cross.shape[0]
-        low = number * PACK
-        own = low + station
-        near = (column > own) & (column <= own + half)
-        sign = jnp.where(column < own, -1.0, 1.0)
-        for pair in range(2):
-            left = jnp.concatenate([diagonal(pair, low), diagonal(pair, low + half)], axis=0)
-            value = product_transposed(left, spectra[pair])
-            rows = slice(pair * 2 * PACK, (pair + 1) * 2 * PACK)
-            for i in range(PACK):
-                first = value[i * 2 * PACK : (i + 1) * 2 * PACK]
-                second = value[(PACK + i) * 2 * PACK : (PACK + i + 1) * 2 * PACK]
-                second = jnp.concatenate([second[:PACK], second[PACK:] * sign[i : i + 1]], axis=0)
-                merged = jnp.where(near[i : i + 1], first, second).astype(jnp.bfloat16)
-                cross[buffer, rows, i * stations : (i + 1) * stations] = merged
-        following = jnp.concatenate(
-            [data_ref[number, 4], data_ref[number + groups // 2, 4]], axis=1
-        ).astype(jnp.float32)
-        shared = pltpu.roll(following, low + 1, 1, stride=1, stride_axis=0)
-        shared = jnp.where(column == own, -1.0, shared)
+    total[...] = jnp.zeros_like(total)
+    for chunk in range(groups // 2):
+        chunk_bins = bins[chunk * PACK : (chunk + 1) * PACK, :]
         hot = []
         for i in range(PACK):
-            value = spread(shared[i : i + 1, :])
+            bin_row = spread(chunk_bins[i : i + 1, :])
             hot.append(
                 jnp.concatenate(
                     [
-                        jnp.where(value == wanted[k : k + PACK], one, zero)
+                        jnp.where(bin_row == wanted[k : k + PACK], one, zero)
                         for k in range(0, bin_count, PACK)
                     ],
                     axis=0,
                 )
             )
-        total[...] += product_transposed(jnp.concatenate(hot, axis=1), cross[buffer])
+        total[...] += product_transposed(jnp.concatenate(hot, axis=1), cross[chunk])
     copies = out_ref.shape[0] // groups
     middle = BIN_DEV // 2
     for group in range(groups):
@@ -524,9 +533,8 @@
             pltpu.VMEM(rows.shape, jnp.float32),
             pltpu.VMEM(small.shape[1:], jnp.float32),
             pltpu.VMEM(tables.shape, jnp.bfloat16),
-            pltpu.VMEM((freq_count + LANES, freq_count), jnp.bfloat16),
             pltpu.VMEM((2, RADIX, station_count * segments, LANES), jnp.float32),
-            pltpu.SemaphoreType.DMA((5,)),
+            pltpu.SemaphoreType.DMA((4,)),
         ],
     )
     received = lax.all_to_all(whitened, "grp", 0, 0, tiled=True)
@@ -537,7 +545,8 @@
         jax.ShapeDtypeStruct((groups * lag_count, BIN_DEV // 2, LANES), jnp.float32),
         [
             pltpu.VMEM((2, stations, 2 * LANES), jnp.bfloat16),
-            pltpu.VMEM((2, 4 * PACK, PACK * stations), jnp.bfloat16),
+            pltpu.VMEM((groups // 2, 4 * PACK, PACK * stations), jnp.bfloat16),
+            pltpu.VMEM((stations // 2, stations), jnp.float32),
             pltpu.VMEM((bin_count, 4 * PACK), jnp.float32),
         ],
     )

time: 40.2 us -> 38.3 us (0.953)
  Pallas kernels: 10.6 us -> 8.72 us
    pallas_call x3, Pallas kernels: 10.6 us -> 8.72 us  [call(): pl.pallas_call(kernel, in_specs=[pl.BlockSpec(memory_space=space) for spa...]
where the time goes in v4:
time: 38.3 us; the launch traced here: 38.1 us
  blocking collectives  29.3 us (77%)
  Pallas kernels  8.72 us (23%)
    all_to_all x1, blocking collectives, local_by_frequency(): received = lax.all_to_all(whitened, 'grp', 0, 0, tiled=True)  19.6 us
    all_to_all x1, blocking collectives, local_by_frequency(): owned = lax.all_to_all(outgoing, ('grp', 'lag'), 0, 0, tiled=True)  9.7 us
    pallas_call x3, Pallas kernels, call(): pl.pallas_call(kernel, in_specs=[pl.BlockSpec(memory_space=space) for spa...  8.72 us

profile of v4, /device:TPU:0, one launch (start us, length us, event | category | flops | bytes accessed | tf_op | source)
XLA Modules:
  0.0 38.1 jit_solution(18006507182754859671)
XLA Ops:
  0.0 3.4 %shard_map.82 = bf16[16,5,16,128]{3,2,1,0:T(8,128)(2,1)S(1)} custom-call(s32[16,256]{1,0:T(8,128)} %bin_hbm.1, f32[128,2048]{1,0:T(8,128)} %bitcast.1, f32[2,16,512]{2,1,0:T(8,128)} %constant.12.clone.small_hbm, bf16[512,640]{1,0:T(8,128)(2,1)} %constant.13.clone.table_hbm), custom_call_target="tpu_custom_call" | custom-call | tf_op jit(solution)/shard_map/pallas_call | solution.py:507
  3.4 0.0 copy-start
  3.4 0.0 copy-start.1
  3.4 19.6 %all_to_all.10.data_ref = bf16[16,5,16,128]{3,2,1,0:T(8,128)(2,1)S(1)} all-to-all(bf16[16,5,16,128]{3,2,1,0:T(8,128)(2,1)S(1)} %shard_map.82), channel_id=1, replica_groups=mesh['grp'=16,'lag'=2] {'grp'}, dimensions={0} | all-to-all | bytes 655360 | tf_op jit(solution)/shard_map/all_to_all | solution.py:540
  23.0 4.2 %shard_map.83 = f32[32,4,128]{2,1,0:T(4,128)S(1)} custom-call(bf16[16,5,16,128]{3,2,1,0:T(8,128)(2,1)S(1)} %all_to_all.10.data_ref), custom_call_target="tpu_custom_call" | custom-call | tf_op jit(solution)/shard_map/pallas_call | solution.py:507
  27.2 0.0 copy-start.2
  27.2 0.0 copy-start.3
  27.2 9.7 %all_to_all.11.data_ref = f32[32,4,128]{2,1,0:T(4,128)S(1)} all-to-all(f32[32,4,128]{2,1,0:T(4,128)S(1)} %shard_map.83), channel_id=1, replica_groups=mesh['grp'=16,'lag'=2] {'grp','lag'}, dimensions={0} | all-to-all | bytes 131072 | tf_op jit(solution)/shard_map/all_to_all | solution.py:553
  36.9 0.0 copy-done
  36.9 0.0 copy-done.1
  36.9 0.0 copy-done.2
  37.0 0.0 copy-done.3
  37.0 1.1 %shard_map.84 = f32[8,512]{1,0:T(8,128)} custom-call(f32[32,4,128]{2,1,0:T(4,128)S(1)} %all_to_all.11.data_ref, bf16[2048,128]{1,0:T(8,128)(2,1)S(1)} %copy-done.1, bf16[2048,128]{1,0:T(8,128)(2,1)S(1)} %copy-done, f32[2,4,2048]{2,1,0:T(4,128)S(1)} %copy-done.3, f32[2,4,2048]{2,1,0:T(4,128)S(1)} %copy-done.2), custom_call_target="tpu_custom_call" | custom-call | tf_op jit(solution)/shard_map/pallas_call | solution.py:507
Async XLA Ops:
  3.4 33.5 %copy-start = (bf16[2048,128]{1,0:T(8,128)(2,1)S(1)}, bf16[2048,128]{1,0:T(8,128)(2,1)}, u32[]{:S(2)}) copy-start(bf16[2048,128]{1,0:T(8,128)(2,1)} %constant.15.clone.low_ref) | copy-start | bytes 1572868
  3.4 33.5 %copy-start.1 = (bf16[2048,128]{1,0:T(8,128)(2,1)S(1)}, bf16[2048,128]{1,0:T(8,128)(2,1)}, u32[]{:S(2)}) copy-start(bf16[2048,128]{1,0:T(8,128)(2,1)} %constant.14.clone.high_ref) | copy-start | bytes 1572868
  27.2 9.7 %copy-start.2 = (f32[2,4,2048]{2,1,0:T(4,128)S(1)}, f32[2,4,2048]{2,1,0:T(4,128)}, u32[]{:S(2)}) copy-start(f32[2,4,2048]{2,1,0:T(4,128)} %constant.17.clone.swapped_ref) | copy-start | bytes 196612
  27.2 9.7 %copy-start.3 = (f32[2,4,2048]{2,1,0:T(4,128)S(1)}, f32[2,4,2048]{2,1,0:T(4,128)}, u32[]{:S(2)}) copy-start(f32[2,4,2048]{2,1,0:T(4,128)} %constant.16.clone.own_ref) | copy-start | bytes 196612

commit v5 on v4

--- a/solution.py
+++ b/solution.py
@@ -169,35 +169,21 @@
     return high, (wide - high.astype(np.float32)).astype(ml_dtypes.bfloat16)
 
 
-def forward_constants(freq_count, lag_count):
-    steps = freq_count // RADIX
+def forward_constants():
+    steps = SPLIT // 2
     sample = np.arange(SPLIT)
-    width = HW // RADIX
-    beyond = np.stack([steps + np.arange(width), np.arange(width) - width])
-    beyond = beyond.reshape(-1)
-    table = np.zeros((SPLIT, 2 * LANES))
-    side = np.zeros((SPLIT, LANES))
     angle = 2.0 * np.pi / SPLIT * (sample[:, None] * np.arange(steps)[None, :] % SPLIT)
-    table[:, :steps] = np.cos(angle)
-    table[:, LANES : LANES + steps] = np.sin(angle)
-    angle = 2.0 * np.pi / SPLIT * (sample[:, None] * beyond[None, :] % SPLIT)
-    side[:, : beyond.size] = np.cos(angle)
-    side[:, LANES // 2 : LANES // 2 + beyond.size] = np.sin(angle)
-    tables = np.concatenate([*halves(table), halves(side)[0]], axis=1)
-    order = np.concatenate([np.arange(steps) * RADIX + r for r in range(RADIX)])
-    small = np.zeros((lag_count, 2 * RADIX + 8, freq_count), np.float32)
-    for index in range(lag_count):
-        start = index * freq_count
-        for r in range(RADIX):
-            angle = 2.0 * np.pi / NFFT * ((start + r) * sample % NFFT)
-            small[index, 2 * r] = np.cos(angle)
-            small[index, 2 * r + 1] = np.sin(angle)
-        upper = np.minimum(start + order + HW, NFFT // 2 - 1)
-        lower = np.maximum(start + order - HW, 0)
-        small[index, 2 * RADIX] = 1.0 / (upper - lower + 1)
-        small[index, 2 * RADIX + 1, :width] = index > 0
-        small[index, 2 * RADIX + 1, LANES - width : LANES] = index < lag_count - 1
-    return small, tables
+    table = np.concatenate([np.cos(angle), np.sin(angle)], axis=1)
+    small = np.zeros((3 * RADIX, SPLIT), np.float32)
+    for r in range(RADIX):
+        angle = 2.0 * np.pi / NFFT * (r * sample % NFFT)
+        small[2 * r] = np.cos(angle)
+        small[2 * r + 1] = np.sin(angle)
+        bins = RADIX * np.arange(steps) + r
+        upper = np.minimum(bins + HW, NFFT // 2 - 1)
+        lower = np.maximum(bins - HW, 0)
+        small[2 * RADIX + r, :steps] = 1.0 / (upper - lower + 1)
+    return small, np.concatenate(halves(table), axis=1)
 
 
 def inverse_constants(freq_count, lag_count, groups):
@@ -245,30 +231,21 @@
     )
 
 
-def whole_steps():
-    reach = HW // RADIX
-    row = lax.broadcasted_iota(jnp.int32, (2 * LANES, LANES), 0)
-    column = lax.broadcasted_iota(jnp.int32, (2 * LANES, LANES), 1)
-    beyond = row - LANES
-    step = jnp.where(beyond < reach, beyond - reach, beyond + reach)
-    step = jnp.where(row < LANES, row, step)
-    inside = (row < LANES) | (beyond < reach) | (beyond >= LANES - reach)
-    near = (jnp.abs(step - column) < reach) & inside
-    return near.astype(jnp.float32).astype(jnp.bfloat16)
-
-
 def whiten_kernel(
     bin_hbm, wave_hbm, small_hbm, table_hbm, out_ref,
     bin_ref, wave_ref, small_ref, table_ref, scratch, sems,
 ):
     rows = wave_ref.shape[0]
-    segments = rows // PACK
-    targets = out_ref.shape[0]
+    owned = bin_ref.shape[0]
+    segments = rows // owned
+    lags = lax.axis_size("lag")
+    targets = out_ref.shape[0] // lags
+    lag = lax.axis_index("lag")
     moves = (
-        (small_hbm.at[lax.axis_index("lag")], small_ref),
-        (wave_hbm, wave_ref),
+        (small_hbm, small_ref),
+        (wave_hbm.at[pl.ds(lag * rows, rows)], wave_ref),
         (table_hbm, table_ref),
-        (bin_hbm, bin_ref),
+        (bin_hbm.at[pl.ds(lag * owned, owned)], bin_ref),
     )
     copies = [
         pltpu.make_async_copy(source, target, sems.at[k])
@@ -276,15 +253,17 @@
     ]
     for copy in copies:
         copy.start()
-    near = whole_steps()
+    steps = table_ref.shape[1] // 4
+    reach = HW // RADIX
+    row = lax.broadcasted_iota(jnp.int32, (steps, steps), 0)
+    column = lax.broadcasted_iota(jnp.int32, (steps, steps), 1)
+    near = jnp.where(jnp.abs(row - column) < reach, 1.0, 0.0).astype(jnp.bfloat16)
     for copy in copies:
         copy.wait()
     quarter = [wave_ref[:, k * SPLIT : (k + 1) * SPLIT] for k in range(RADIX)]
     even_sum, odd_sum = quarter[0] + quarter[2], quarter[1] + quarter[3]
     even, odd = quarter[0] - quarter[2], quarter[1] - quarter[3]
-    main, rest = slice(0, 2 * LANES), slice(2 * LANES, 4 * LANES)
-    side = slice(4 * LANES, 5 * LANES)
-    spectra, amplitudes, outside = [], [], []
+    high, low = [], []
     for r, first, second in (
         (0, even_sum + odd_sum, None), (1, even, -odd), (2, even_sum - odd_sum, None), (3, even, odd)
     ):
@@ -293,83 +272,108 @@
         if second is not None:
             turned_real = turned_real + second * sine
             turned_imag = turned_imag + second * cosine
-        high, low = split_float(jnp.concatenate([turned_real, turned_imag], axis=0))
-        value = product(high, table_ref[:, main]) + product(low, table_ref[:, main])
-        value = value + product(high, table_ref[:, rest])
-        beyond = product(high, table_ref[:, side])
-        real = value[:rows, :LANES] + value[rows:, LANES:]
-        imag = value[rows:, :LANES] - value[:rows, LANES:]
+        for turned in (turned_real, turned_imag):
+            turned_high, turned_low = split_float(turned)
+            high.append(turned_high)
+            low.append(turned_low)
+    high = jnp.concatenate(high, axis=0)
+    low = jnp.concatenate(low, axis=0)
+    table_high, table_low = table_ref[:, : 2 * steps], table_ref[:, 2 * steps :]
+    value = product(high, table_high) + product(low, table_high) + product(high, table_low)
+    spectra, amplitudes = [], []
+    for r in range(RADIX):
+        first = value[2 * r * rows : (2 * r + 1) * rows]
+        second = value[(2 * r + 1) * rows : (2 * r + 2) * rows]
+        real = first[:, :steps] + second[:, steps:]
+        imag = second[:, :steps] - first[:, steps:]
         spectra.append((real, imag))
         amplitudes.append(jnp.sqrt(real * real + imag * imag))
-        real = beyond[:rows] + pltpu.roll(beyond[rows:], LANES // 2, 1)
-        imag = beyond[rows:] - pltpu.roll(beyond[:rows], LANES // 2, 1)
-        outside.append(jnp.sqrt(real * real + imag * imag))
-    reach = HW // RADIX
-    there = small_ref[2 * RADIX + 1 : 2 * RADIX + 2, :LANES]
-    outside = [pltpu.roll(value, LANES - reach, 1) * there for value in outside]
-    sums = jnp.concatenate([sum(amplitudes), sum(outside)], axis=1)
-    sums_high, sums_low = split_float(sums)
+    sums_high, sums_low = split_float(sum(amplitudes))
     common = product(sums_high, near) + product(sums_low, near)
-    lane = lax.broadcasted_iota(jnp.int32, (rows, LANES), 1)
+    step = lax.broadcasted_iota(jnp.int32, (rows, steps), 1)
     for r, (real, imag) in enumerate(spectra):
-        above = pltpu.roll(sum(amplitudes[: r + 1]), LANES - reach, 1)
-        above = jnp.where(lane < LANES - reach, above, sum(outside[: r + 1]))
+        above = pltpu.roll(sum(amplitudes[: r + 1]), steps - reach, 1)
+        above = jnp.where(step < steps - reach, above, 0.0)
         below = pltpu.roll(sum(amplitudes[r:]), reach, 1)
-        below = jnp.where(lane >= reach, below, sum(outside[r:]))
-        count = small_ref[2 * RADIX : 2 * RADIX + 1, r * LANES : (r + 1) * LANES]
+        below = jnp.where(step >= reach, below, 0.0)
+        count = small_ref[2 * RADIX + r : 2 * RADIX + r + 1, :steps]
         scale = 1.0 / ((common + above + below) * count + EPSILON)
-        scratch[0, r] = real * scale
-        scratch[1, r] = imag * scale
+        for tile in range(lags):
+            at = slice(tile * LANES, (tile + 1) * LANES)
+            scratch[0, r, tile] = real[:, at] * scale[:, at]
+            scratch[1, r, tile] = imag[:, at] * scale[:, at]
     stations = bin_ref.shape[1]
+    first_station = lax.axis_index("grp") * PACK + lag * owned
     turned = pltpu.roll(
-        bin_ref[...].astype(jnp.float32), (stations - lax.axis_index("grp") * PACK) % stations, 1
+        bin_ref[...].astype(jnp.float32), (stations - first_station) % stations, 1
     )
     following = jnp.concatenate(
         [
             pltpu.roll(turned[i : i + 1, :], stations - 1 - i, 1)[:, : stations // 2]
-            for i in range(PACK)
+            for i in range(owned)
         ],
         axis=0,
     ).astype(jnp.bfloat16)
     width = LANES // targets
     chunk = lax.broadcasted_iota(jnp.int32, (PACK, LANES), 1) // width
-    chunk = chunk.astype(jnp.float32).astype(jnp.bfloat16)
-    masks = [chunk == jnp.bfloat16(place) for place in range(targets)]
+    bits = []
+    while 2 ** len(bits) < targets:
+        odd_chunk = chunk // 2 ** len(bits) % 2
+        bits.append(odd_chunk.astype(jnp.float32).astype(jnp.bfloat16) == jnp.bfloat16(1))
     for pair in range(2):
-        for part in range(2):
-            rolled = []
+        for tile in range(lags):
+            tiles = []
             for half in range(2):
                 for segment in range(segments):
-                    rows_of = scratch[part, 2 * pair + half, pl.ds(segment, PACK, stride=segments), :]
+                    at = pl.ds(segment, owned, stride=segments)
+                    both = jnp.concatenate(
+                        [scratch[part, 2 * pair + half, tile, at, :] for part in range(2)], axis=0
+                    )
                     shift = width * (half * segments + segment)
-                    rows_of = pltpu.roll(rows_of, shift, 1) if shift else rows_of
-                    rolled.append(rows_of.astype(jnp.bfloat16))
+                    both = pltpu.roll(both, shift, 1) if shift else both
+                    tiles.append(both.astype(jnp.bfloat16))
+            for bit, mask in enumerate(bits):
+                tiles = [
+                    jnp.where(mask, tiles[(k + 2**bit) % targets], tiles[k])
+                    for k in range(targets)
+                ]
             for target in range(targets):
-                value = rolled[-target % targets]
-                for place in range(1, targets):
-                    value = jnp.where(masks[place], rolled[(place - target) % targets], value)
-                out_ref[target, 2 * pair + part] = value
-    for target in range(targets):
-        out_ref[target, 4] = following
+                out_ref[target * lags + tile, pair * PACK : (pair + 1) * PACK, :] = tiles[
+                    -target % targets
+                ]
+    for target in range(targets * lags):
+        out_ref[target, 2 * PACK :, :] = following
 
 
 def pair_kernel(data_ref, out_ref, spectra, cross, bins, total):
-    groups = data_ref.shape[0]
+    groups = lax.axis_size("grp")
     stations = groups * PACK
     bin_count = total.shape[0]
     width = LANES // groups
     half = stations // 2
+    shares = data_ref.shape[0] // groups
+    owned = PACK // shares
+
+    def gathered(group, first_row):
+        return jnp.concatenate(
+            [
+                data_ref[group * shares + k, first_row : first_row + owned, :]
+                for k in range(shares)
+            ],
+            axis=0,
+        )
+
     for group in range(groups):
         for pair in range(2):
             for part in range(2):
                 spectra[
                     pair, group * PACK : (group + 1) * PACK, part * LANES : (part + 1) * LANES
-                ] = data_ref[group, 2 * pair + part]
+                ] = gathered(group, pair * PACK + part * owned)
     station = lax.broadcasted_iota(jnp.int32, (half, half), 0)
     column = lax.broadcasted_iota(jnp.int32, (half, half), 1)
     for group in range(groups // 2):
         following = jnp.concatenate(
-            [data_ref[group, 4], data_ref[group + groups // 2, 4]], axis=1
+            [gathered(group, 2 * PACK), gathered(group + groups // 2, 2 * PACK)], axis=1
         ).astype(jnp.float32)
         bins[group * PACK : (group + 1) * PACK, :] = pltpu.roll(
             following, group * PACK + 1, 1, stride=1, stride_axis=0
@@ -522,22 +526,23 @@
     stations = station_count * groups
     bin_count = BIN_DEV * groups
     rows = waveforms.reshape(station_count * segments, NFFT)
-    small, tables = [jnp.asarray(t) for t in forward_constants(freq_count, lag_count)]
+    small, table = [jnp.asarray(t) for t in forward_constants()]
+    owned = station_count // lag_count
     whitened = call(
         whiten_kernel,
-        [pair_bin, rows, small, tables],
+        [pair_bin, rows, small, table],
         [pltpu.HBM] * 4,
-        jax.ShapeDtypeStruct((groups, 5, PACK, LANES), jnp.bfloat16),
+        jax.ShapeDtypeStruct((groups * lag_count, 2 * PACK + owned, LANES), jnp.bfloat16),
         [
-            pltpu.VMEM(pair_bin.shape, jnp.int32),
-            pltpu.VMEM(rows.shape, jnp.float32),
-            pltpu.VMEM(small.shape[1:], jnp.float32),
-            pltpu.VMEM(tables.shape, jnp.bfloat16),
-            pltpu.VMEM((2, RADIX, station_count * segments, LANES), jnp.float32),
+            pltpu.VMEM((owned, stations), jnp.int32),
+            pltpu.VMEM((owned * segments, NFFT), jnp.float32),
+            pltpu.VMEM(small.shape, jnp.float32),
+            pltpu.VMEM(table.shape, jnp.bfloat16),
+            pltpu.VMEM((2, RADIX, lag_count, owned * segments, LANES), jnp.float32),
             pltpu.SemaphoreType.DMA((4,)),
         ],
     )
-    received = lax.all_to_all(whitened, "grp", 0, 0, tiled=True)
+    received = lax.all_to_all(whitened, ("grp", "lag"), 0, 0, tiled=True)
     outgoing = call(
         pair_kernel,
         [received],

time: 38.3 us -> 37.3 us (0.974)
  blocking collectives: 29.3 us -> 28.7 us
  Pallas kernels: 8.72 us -> 8.25 us
    all_to_all x1, blocking collectives: 19.6 us -> 19.1 us  [local_by_frequency(): received = lax.all_to_all(whitened, ('grp', 'lag'), 0, 0, tiled=True)]
    pallas_call x3, Pallas kernels: 8.72 us -> 8.25 us  [call(): pl.pallas_call(kernel, in_specs=[pl.BlockSpec(memory_space=space) for spa...]
where the time goes in v5:
time: 37.3 us; the launch traced here: 37.1 us
  blocking collectives  28.7 us (77%)
  Pallas kernels  8.25 us (22%)
    all_to_all x1, blocking collectives, local_by_frequency(): received = lax.all_to_all(whitened, ('grp', 'lag'), 0, 0, tiled=True)  19.1 us
    all_to_all x1, blocking collectives, local_by_frequency(): owned = lax.all_to_all(outgoing, ('grp', 'lag'), 0, 0, tiled=True)  9.64 us
    pallas_call x3, Pallas kernels, call(): pl.pallas_call(kernel, in_specs=[pl.BlockSpec(memory_space=space) for spa...  8.25 us

profile of v5, /device:TPU:0, one launch (start us, length us, event | category | flops | bytes accessed | tf_op | source)
XLA Modules:
  0.0 37.1 jit_solution(445117038035265498)
XLA Ops:
  0.0 3.0 %shard_map.82 = bf16[32,40,128]{2,1,0:T(8,128)(2,1)S(1)} custom-call(s32[16,256]{1,0:T(8,128)} %bin_hbm.1, f32[128,2048]{1,0:T(8,128)} %bitcast.1, f32[12,512]{1,0:T(8,128)} %constant.12.clone.small_hbm, bf16[512,1024]{1,0:T(8,128)(2,1)} %constant.13.clone.table_hbm), custom_call_target="tpu_custom_call" | custom-call | tf_op jit(solution)/shard_map/pallas_call | solution.py:511
  3.0 0.0 copy-start
  3.0 0.0 copy-start.1
  3.0 19.1 %all_to_all.10.data_ref = bf16[32,40,128]{2,1,0:T(8,128)(2,1)S(1)} all-to-all(bf16[32,40,128]{2,1,0:T(8,128)(2,1)S(1)} %shard_map.82), channel_id=1, replica_groups=mesh['grp'=16,'lag'=2] {'grp','lag'}, dimensions={0} | all-to-all | bytes 655360 | tf_op jit(solution)/shard_map/all_to_all | solution.py:545
  22.1 4.2 %shard_map.83 = f32[32,4,128]{2,1,0:T(4,128)S(1)} custom-call(bf16[32,40,128]{2,1,0:T(8,128)(2,1)S(1)} %all_to_all.10.data_ref), custom_call_target="tpu_custom_call" | custom-call | tf_op jit(solution)/shard_map/pallas_call | solution.py:511
  26.3 0.0 copy-start.2
  26.3 0.0 copy-start.3
  26.3 9.6 %all_to_all.11.data_ref = f32[32,4,128]{2,1,0:T(4,128)S(1)} all-to-all(f32[32,4,128]{2,1,0:T(4,128)S(1)} %shard_map.83), channel_id=1, replica_groups=mesh['grp'=16,'lag'=2] {'grp','lag'}, dimensions={0} | all-to-all | bytes 131072 | tf_op jit(solution)/shard_map/all_to_all | solution.py:558
  35.9 0.0 copy-done
  35.9 0.0 copy-done.1
  35.9 0.0 copy-done.2
  36.0 0.0 copy-done.3
  36.0 1.1 %shard_map.84 = f32[8,512]{1,0:T(8,128)} custom-call(f32[32,4,128]{2,1,0:T(4,128)S(1)} %all_to_all.11.data_ref, bf16[2048,128]{1,0:T(8,128)(2,1)S(1)} %copy-done.1, bf16[2048,128]{1,0:T(8,128)(2,1)S(1)} %copy-done, f32[2,4,2048]{2,1,0:T(4,128)S(1)} %copy-done.3, f32[2,4,2048]{2,1,0:T(4,128)S(1)} %copy-done.2), custom_call_target="tpu_custom_call" | custom-call | tf_op jit(solution)/shard_map/pallas_call | solution.py:511
Async XLA Ops:
  3.0 33.0 %copy-start = (bf16[2048,128]{1,0:T(8,128)(2,1)S(1)}, bf16[2048,128]{1,0:T(8,128)(2,1)}, u32[]{:S(2)}) copy-start(bf16[2048,128]{1,0:T(8,128)(2,1)} %constant.15.clone.low_ref) | copy-start | bytes 1572868
  3.0 33.0 %copy-start.1 = (bf16[2048,128]{1,0:T(8,128)(2,1)S(1)}, bf16[2048,128]{1,0:T(8,128)(2,1)}, u32[]{:S(2)}) copy-start(bf16[2048,128]{1,0:T(8,128)(2,1)} %constant.14.clone.high_ref) | copy-start | bytes 1572868
  26.3 9.7 %copy-start.2 = (f32[2,4,2048]{2,1,0:T(4,128)S(1)}, f32[2,4,2048]{2,1,0:T(4,128)}, u32[]{:S(2)}) copy-start(f32[2,4,2048]{2,1,0:T(4,128)} %constant.17.clone.swapped_ref) | copy-start | bytes 196612
  26.3 9.7 %copy-start.3 = (f32[2,4,2048]{2,1,0:T(4,128)S(1)}, f32[2,4,2048]{2,1,0:T(4,128)}, u32[]{:S(2)}) copy-start(f32[2,4,2048]{2,1,0:T(4,128)} %constant.16.clone.own_ref) | copy-start | bytes 196612

commit v6 on v5

--- a/solution.py
+++ b/solution.py
@@ -158,7 +158,7 @@
 
 
 LANES = 128
-RADIX = 4
+RADIX = 8
 SPLIT = NFFT // RADIX
 PACK = 16
 
@@ -186,13 +186,13 @@
     return small, np.concatenate(halves(table), axis=1)
 
 
-def inverse_constants(freq_count, lag_count, groups):
-    run = freq_count // groups
-    quarter = run // RADIX
-    index = np.arange(groups * lag_count)
-    start = (index % lag_count) * freq_count + (index // lag_count) * run
-    pair, half, step = np.meshgrid(np.arange(2), np.arange(2), np.arange(quarter), indexing="ij")
-    offset = (RADIX * step + 2 * pair + half).reshape(2, PACK)
+def inverse_constants(lag_count, groups):
+    run = NFFT // 2 // (groups * lag_count)
+    start = np.arange(groups * lag_count) * run
+    pair, half, step = np.meshgrid(
+        np.arange(2), np.arange(RADIX // 2), np.arange(run // RADIX), indexing="ij"
+    )
+    offset = (RADIX * step + RADIX // 2 * pair + half).reshape(2, PACK)
     bins = start[:, None, None] + offset[None]
     both = np.stack([bins, bins], axis=2)
     imaginary = np.stack([np.zeros_like(bins), np.ones_like(bins)], axis=2).reshape(-1)
@@ -238,8 +238,7 @@
     rows = wave_ref.shape[0]
     owned = bin_ref.shape[0]
     segments = rows // owned
-    lags = lax.axis_size("lag")
-    targets = out_ref.shape[0] // lags
+    targets = out_ref.shape[0]
     lag = lax.axis_index("lag")
     moves = (
         (small_hbm, small_ref),
@@ -260,13 +259,24 @@
     near = jnp.where(jnp.abs(row - column) < reach, 1.0, 0.0).astype(jnp.bfloat16)
     for copy in copies:
         copy.wait()
-    quarter = [wave_ref[:, k * SPLIT : (k + 1) * SPLIT] for k in range(RADIX)]
-    even_sum, odd_sum = quarter[0] + quarter[2], quarter[1] + quarter[3]
-    even, odd = quarter[0] - quarter[2], quarter[1] - quarter[3]
+    part = [wave_ref[:, k * SPLIT : (k + 1) * SPLIT] for k in range(RADIX)]
+    sums = [part[k] + part[k + 4] for k in range(4)]
+    gaps = [part[k] - part[k + 4] for k in range(4)]
+    even, odd = sums[0] + sums[2], sums[1] + sums[3]
+    even_gap, odd_gap = sums[0] - sums[2], sums[1] - sums[3]
+    across, along = math.sqrt(0.5) * (gaps[1] - gaps[3]), math.sqrt(0.5) * (gaps[1] + gaps[3])
+    folded = (
+        (even + odd, None),
+        (gaps[0] + across, -gaps[2] - along),
+        (even_gap, -odd_gap),
+        (gaps[0] - across, gaps[2] - along),
+        (even - odd, None),
+        (gaps[0] - across, along - gaps[2]),
+        (even_gap, odd_gap),
+        (gaps[0] + across, gaps[2] + along),
+    )
     high, low = [], []
-    for r, first, second in (
-        (0, even_sum + odd_sum, None), (1, even, -odd), (2, even_sum - odd_sum, None), (3, even, odd)
-    ):
+    for r, (first, second) in enumerate(folded):
         cosine, sine = small_ref[2 * r : 2 * r + 1, :], small_ref[2 * r + 1 : 2 * r + 2, :]
         turned_real, turned_imag = first * cosine, -first * sine
         if second is not None:
@@ -298,10 +308,8 @@
         below = jnp.where(step >= reach, below, 0.0)
         count = small_ref[2 * RADIX + r : 2 * RADIX + r + 1, :steps]
         scale = 1.0 / ((common + above + below) * count + EPSILON)
-        for tile in range(lags):
-            at = slice(tile * LANES, (tile + 1) * LANES)
-            scratch[0, r, tile] = real[:, at] * scale[:, at]
-            scratch[1, r, tile] = imag[:, at] * scale[:, at]
+        scratch[0, r] = real * scale
+        scratch[1, r] = imag * scale
     stations = bin_ref.shape[1]
     first_station = lax.axis_index("grp") * PACK + lag * owned
     turned = pltpu.roll(
@@ -321,27 +329,23 @@
         odd_chunk = chunk // 2 ** len(bits) % 2
         bits.append(odd_chunk.astype(jnp.float32).astype(jnp.bfloat16) == jnp.bfloat16(1))
     for pair in range(2):
-        for tile in range(lags):
-            tiles = []
-            for half in range(2):
-                for segment in range(segments):
-                    at = pl.ds(segment, owned, stride=segments)
-                    both = jnp.concatenate(
-                        [scratch[part, 2 * pair + half, tile, at, :] for part in range(2)], axis=0
-                    )
-                    shift = width * (half * segments + segment)
-                    both = pltpu.roll(both, shift, 1) if shift else both
-                    tiles.append(both.astype(jnp.bfloat16))
-            for bit, mask in enumerate(bits):
-                tiles = [
-                    jnp.where(mask, tiles[(k + 2**bit) % targets], tiles[k])
-                    for k in range(targets)
-                ]
-            for target in range(targets):
-                out_ref[target * lags + tile, pair * PACK : (pair + 1) * PACK, :] = tiles[
-                    -target % targets
-                ]
-    for target in range(targets * lags):
+        tiles = []
+        for half in range(RADIX // 2):
+            for segment in range(segments):
+                at = pl.ds(segment, owned, stride=segments)
+                both = jnp.concatenate(
+                    [scratch[k, RADIX // 2 * pair + half, at, :] for k in range(2)], axis=0
+                )
+                shift = width * (half * segments + segment)
+                both = pltpu.roll(both, shift, 1) if shift else both
+                tiles.append(both.astype(jnp.bfloat16))
+        for bit, mask in enumerate(bits):
+            tiles = [
+                jnp.where(mask, tiles[(k + 2**bit) % targets], tiles[k]) for k in range(targets)
+            ]
+        for target in range(targets):
+            out_ref[target, pair * PACK : (pair + 1) * PACK, :] = tiles[-target % targets]
+    for target in range(targets):
         out_ref[target, 2 * PACK :, :] = following
 
 
@@ -349,7 +353,7 @@
     groups = lax.axis_size("grp")
     stations = groups * PACK
     bin_count = total.shape[0]
-    width = LANES // groups
+    width = LANES // data_ref.shape[0]
     half = stations // 2
     shares = data_ref.shape[0] // groups
     owned = PACK // shares
@@ -394,8 +398,9 @@
 
     lane = lax.broadcasted_iota(jnp.int32, (PACK, 2 * LANES), 1)
     row = lax.broadcasted_iota(jnp.int32, (PACK, 2 * LANES), 0)
-    place = (lane % LANES // width - lax.axis_index("grp") + groups) % groups
-    slot = place // (groups // 2) * width + lane % width
+    position = lax.axis_index("grp") * shares + lax.axis_index("lag")
+    place = (lane % LANES // width - position + shares * groups) % (shares * groups)
+    slot = place // (LANES // PACK) * width + lane % width
     sign = jnp.where(lane < LANES, -1.0, 1.0)
     keep = as_float(slot == row)
     keep_own = keep.astype(jnp.bfloat16)
@@ -522,7 +527,6 @@
     station_count, segments, _ = waveforms.shape
     groups = lax.axis_size("grp")
     lag_count = lax.axis_size("lag")
-    freq_count = NFFT // 2 // lag_count
     stations = station_count * groups
     bin_count = BIN_DEV * groups
     rows = waveforms.reshape(station_count * segments, NFFT)
@@ -538,7 +542,7 @@
             pltpu.VMEM((owned * segments, NFFT), jnp.float32),
             pltpu.VMEM(small.shape, jnp.float32),
             pltpu.VMEM(table.shape, jnp.bfloat16),
-            pltpu.VMEM((2, RADIX, lag_count, owned * segments, LANES), jnp.float32),
+            pltpu.VMEM((2, RADIX, owned * segments, LANES), jnp.float32),
             pltpu.SemaphoreType.DMA((4,)),
         ],
     )
@@ -557,7 +561,7 @@
     )
     owned = lax.all_to_all(outgoing, ("grp", "lag"), 0, 0, tiled=True)
     high, low, own, swapped = [
-        jnp.asarray(t) for t in inverse_constants(freq_count, lag_count, groups)
+        jnp.asarray(t) for t in inverse_constants(lag_count, groups)
     ]
     return call(
         lag_kernel,
@@ -570,12 +574,11 @@
 def fits_by_frequency(mesh, waveforms):
     groups, lag_count = mesh.shape["grp"], mesh.shape["lag"]
     stations, segments, _ = waveforms.shape
-    freq_count = NFFT // 2 // lag_count
     return (
         lag_count == 2
         and stations == groups * PACK == 2 * LANES
-        and freq_count == RADIX * LANES
-        and segments * 2 * (LANES // groups) == LANES
+        and segments * PACK == LANES
+        and groups * lag_count * 2 * PACK == NFFT // 2 == RADIX * LANES
         and groups * BIN_DEV <= 256
     )
 

time: 37.3 us -> 36.5 us (0.979)
  Pallas kernels: 8.25 us -> 7.47 us
    pallas_call x3, Pallas kernels: 8.25 us -> 7.47 us  [call(): pl.pallas_call(kernel, in_specs=[pl.BlockSpec(memory_space=space) for spa...]
where the time goes in v6:
time: 36.5 us; the launch traced here: 36.3 us
  blocking collectives  28.7 us (79%)
  Pallas kernels  7.47 us (20%)
    all_to_all x1, blocking collectives, local_by_frequency(): received = lax.all_to_all(whitened, ('grp', 'lag'), 0, 0, tiled=True)  19.1 us
    all_to_all x1, blocking collectives, local_by_frequency(): owned = lax.all_to_all(outgoing, ('grp', 'lag'), 0, 0, tiled=True)  9.63 us
    pallas_call x3, Pallas kernels, call(): pl.pallas_call(kernel, in_specs=[pl.BlockSpec(memory_space=space) for spa...  7.47 us

profile of v6, /device:TPU:0, one launch (start us, length us, event | category | flops | bytes accessed | tf_op | source)
XLA Modules:
  0.0 36.3 jit_solution(8389596628864600450)
XLA Ops:
  0.0 2.2 %shard_map.82 = bf16[32,40,128]{2,1,0:T(8,128)(2,1)S(1)} custom-call(s32[16,256]{1,0:T(8,128)} %bin_hbm.1, f32[128,2048]{1,0:T(8,128)} %bitcast.1, f32[24,256]{1,0:T(8,128)} %constant.12.clone.small_hbm, bf16[256,512]{1,0:T(8,128)(2,1)} %constant.13.clone.table_hbm), custom_call_target="tpu_custom_call" | custom-call | tf_op jit(solution)/shard_map/pallas_call | solution.py:516
  2.2 0.0 copy-start
  2.2 0.0 copy-start.1
  2.2 19.1 %all_to_all.10.data_ref = bf16[32,40,128]{2,1,0:T(8,128)(2,1)S(1)} all-to-all(bf16[32,40,128]{2,1,0:T(8,128)(2,1)S(1)} %shard_map.82), channel_id=1, replica_groups=mesh['grp'=16,'lag'=2] {'grp','lag'}, dimensions={0} | all-to-all | bytes 655360 | tf_op jit(solution)/shard_map/all_to_all | solution.py:549
  21.3 4.2 %shard_map.83 = f32[32,4,128]{2,1,0:T(4,128)S(1)} custom-call(bf16[32,40,128]{2,1,0:T(8,128)(2,1)S(1)} %all_to_all.10.data_ref), custom_call_target="tpu_custom_call" | custom-call | tf_op jit(solution)/shard_map/pallas_call | solution.py:516
  25.5 0.0 copy-start.2
  25.5 0.0 copy-start.3
  25.5 9.6 %all_to_all.11.data_ref = f32[32,4,128]{2,1,0:T(4,128)S(1)} all-to-all(f32[32,4,128]{2,1,0:T(4,128)S(1)} %shard_map.83), channel_id=1, replica_groups=mesh['grp'=16,'lag'=2] {'grp','lag'}, dimensions={0} | all-to-all | bytes 131072 | tf_op jit(solution)/shard_map/all_to_all | solution.py:562
  35.2 0.0 copy-done
  35.2 0.0 copy-done.1
  35.2 0.0 copy-done.2
  35.2 0.0 copy-done.3
  35.2 1.1 %shard_map.84 = f32[8,512]{1,0:T(8,128)} custom-call(f32[32,4,128]{2,1,0:T(4,128)S(1)} %all_to_all.11.data_ref, bf16[2048,128]{1,0:T(8,128)(2,1)S(1)} %copy-done.1, bf16[2048,128]{1,0:T(8,128)(2,1)S(1)} %copy-done, f32[2,4,2048]{2,1,0:T(4,128)S(1)} %copy-done.3, f32[2,4,2048]{2,1,0:T(4,128)S(1)} %copy-done.2), custom_call_target="tpu_custom_call" | custom-call | tf_op jit(solution)/shard_map/pallas_call | solution.py:516
Async XLA Ops:
  2.2 33.0 %copy-start = (bf16[2048,128]{1,0:T(8,128)(2,1)S(1)}, bf16[2048,128]{1,0:T(8,128)(2,1)}, u32[]{:S(2)}) copy-start(bf16[2048,128]{1,0:T(8,128)(2,1)} %constant.15.clone.low_ref) | copy-start | bytes 1572868
  2.2 33.0 %copy-start.1 = (bf16[2048,128]{1,0:T(8,128)(2,1)S(1)}, bf16[2048,128]{1,0:T(8,128)(2,1)}, u32[]{:S(2)}) copy-start(bf16[2048,128]{1,0:T(8,128)(2,1)} %constant.14.clone.high_ref) | copy-start | bytes 1572868
  25.5 9.7 %copy-start.2 = (f32[2,4,2048]{2,1,0:T(4,128)S(1)}, f32[2,4,2048]{2,1,0:T(4,128)}, u32[]{:S(2)}) copy-start(f32[2,4,2048]{2,1,0:T(4,128)} %constant.17.clone.swapped_ref) | copy-start | bytes 196612
  25.5 9.7 %copy-start.3 = (f32[2,4,2048]{2,1,0:T(4,128)S(1)}, f32[2,4,2048]{2,1,0:T(4,128)}, u32[]{:S(2)}) copy-start(f32[2,4,2048]{2,1,0:T(4,128)} %constant.16.clone.own_ref) | copy-start | bytes 196612

commit v7 on v6

--- a/solution.py
+++ b/solution.py
@@ -448,7 +448,6 @@
     wanted = lax.broadcasted_iota(jnp.int32, (bin_count, stations), 0).astype(jnp.float32)
     wanted = wanted.astype(jnp.bfloat16)
     one, zero = jnp.bfloat16(1), jnp.bfloat16(0)
-    total[...] = jnp.zeros_like(total)
     for chunk in range(groups // 2):
         chunk_bins = bins[chunk * PACK : (chunk + 1) * PACK, :]
         hot = []
@@ -463,7 +462,8 @@
                     axis=0,
                 )
             )
-        total[...] += product_transposed(jnp.concatenate(hot, axis=1), cross[chunk])
+        added = product_transposed(jnp.concatenate(hot, axis=1), cross[chunk])
+        total[...] = total[...] + added if chunk else added
     copies = out_ref.shape[0] // groups
     middle = BIN_DEV // 2
     for group in range(groups):
@@ -502,8 +502,12 @@
             )
     left = jnp.concatenate([jnp.concatenate(row, axis=1) for row in turned], axis=0)
     left_high, left_low = split_float(left)
-    value = product(left_high, high_ref[...]) + product(left_low, high_ref[...])
-    value = value + product(left_high, low_ref[...])
+    rows = blocks * owned
+    value = product(
+        jnp.concatenate([left_high, left_low], axis=0),
+        jnp.concatenate([high_ref[...], low_ref[...]], axis=1),
+    )
+    value = value[:rows, :LANES] + value[:rows, LANES:] + value[rows:, :LANES]
     for block in range(blocks):
         out_ref[:, block * LANES : (block + 1) * LANES] = value[block * owned : (block + 1) * owned]
 

time: 36.5 us -> 36.4 us (level)
  no operation moved by 1% of the time
where the time goes in v7:
time: 36.4 us; the launch traced here: 36.2 us
  blocking collectives  28.7 us (79%)
  Pallas kernels  7.4 us (20%)
    all_to_all x1, blocking collectives, local_by_frequency(): received = lax.all_to_all(whitened, ('grp', 'lag'), 0, 0, tiled=True)  19.1 us
    all_to_all x1, blocking collectives, local_by_frequency(): owned = lax.all_to_all(outgoing, ('grp', 'lag'), 0, 0, tiled=True)  9.64 us
    pallas_call x3, Pallas kernels, call(): pl.pallas_call(kernel, in_specs=[pl.BlockSpec(memory_space=space) for spa...  7.4 us

profile of v7, /device:TPU:0, one launch (start us, length us, event | category | flops | bytes accessed | tf_op | source)
XLA Modules:
  0.0 36.2 jit_solution(18339501035853149070)
XLA Ops:
  0.0 2.2 %shard_map.82 = bf16[32,40,128]{2,1,0:T(8,128)(2,1)S(1)} custom-call(s32[16,256]{1,0:T(8,128)} %bin_hbm.1, f32[128,2048]{1,0:T(8,128)} %bitcast.1, f32[24,256]{1,0:T(8,128)} %constant.12.clone.small_hbm, bf16[256,512]{1,0:T(8,128)(2,1)} %constant.13.clone.table_hbm), custom_call_target="tpu_custom_call" | custom-call | tf_op jit(solution)/shard_map/pallas_call | solution.py:520
  2.2 0.0 copy-start
  2.2 0.0 copy-start.1
  2.2 19.1 %all_to_all.10.data_ref = bf16[32,40,128]{2,1,0:T(8,128)(2,1)S(1)} all-to-all(bf16[32,40,128]{2,1,0:T(8,128)(2,1)S(1)} %shard_map.82), channel_id=1, replica_groups=mesh['grp'=16,'lag'=2] {'grp','lag'}, dimensions={0} | all-to-all | bytes 655360 | tf_op jit(solution)/shard_map/all_to_all | solution.py:553
  21.3 4.2 %shard_map.83 = f32[32,4,128]{2,1,0:T(4,128)S(1)} custom-call(bf16[32,40,128]{2,1,0:T(8,128)(2,1)S(1)} %all_to_all.10.data_ref), custom_call_target="tpu_custom_call" | custom-call | tf_op jit(solution)/shard_map/pallas_call | solution.py:520
  25.5 0.0 copy-start.2
  25.5 0.0 copy-start.3
  25.5 9.6 %all_to_all.11.data_ref = f32[32,4,128]{2,1,0:T(4,128)S(1)} all-to-all(f32[32,4,128]{2,1,0:T(4,128)S(1)} %shard_map.83), channel_id=1, replica_groups=mesh['grp'=16,'lag'=2] {'grp','lag'}, dimensions={0} | all-to-all | bytes 131072 | tf_op jit(solution)/shard_map/all_to_all | solution.py:566
  35.2 0.0 copy-done
  35.2 0.0 copy-done.1
  35.2 0.0 copy-done.2
  35.2 0.0 copy-done.3
  35.2 1.0 %shard_map.84 = f32[8,512]{1,0:T(8,128)} custom-call(f32[32,4,128]{2,1,0:T(4,128)S(1)} %all_to_all.11.data_ref, bf16[2048,128]{1,0:T(8,128)(2,1)S(1)} %copy-done.1, bf16[2048,128]{1,0:T(8,128)(2,1)S(1)} %copy-done, f32[2,4,2048]{2,1,0:T(4,128)S(1)} %copy-done.3, f32[2,4,2048]{2,1,0:T(4,128)S(1)} %copy-done.2), custom_call_target="tpu_custom_call" | custom-call | tf_op jit(solution)/shard_map/pallas_call | solution.py:520
Async XLA Ops:
  2.2 33.0 %copy-start = (bf16[2048,128]{1,0:T(8,128)(2,1)S(1)}, bf16[2048,128]{1,0:T(8,128)(2,1)}, u32[]{:S(2)}) copy-start(bf16[2048,128]{1,0:T(8,128)(2,1)} %constant.15.clone.low_ref) | copy-start | bytes 1572868
  2.2 33.0 %copy-start.1 = (bf16[2048,128]{1,0:T(8,128)(2,1)S(1)}, bf16[2048,128]{1,0:T(8,128)(2,1)}, u32[]{:S(2)}) copy-start(bf16[2048,128]{1,0:T(8,128)(2,1)} %constant.14.clone.high_ref) | copy-start | bytes 1572868
  25.5 9.7 %copy-start.2 = (f32[2,4,2048]{2,1,0:T(4,128)S(1)}, f32[2,4,2048]{2,1,0:T(4,128)}, u32[]{:S(2)}) copy-start(f32[2,4,2048]{2,1,0:T(4,128)} %constant.17.clone.swapped_ref) | copy-start | bytes 196612
  25.5 9.7 %copy-start.3 = (f32[2,4,2048]{2,1,0:T(4,128)S(1)}, f32[2,4,2048]{2,1,0:T(4,128)}, u32[]{:S(2)}) copy-start(f32[2,4,2048]{2,1,0:T(4,128)} %constant.16.clone.own_ref) | copy-start | bytes 196612
